TPU v7x, 512 devices: a whole 4x4x16 slice. The times are simulated.
512 devices in a mesh: row: 32 (over z, core), col: 16 (over y, x).
Axes of the slice: x: 4, y: 4, z: 16, core: 2. Of those that a mesh axis runs over, the one named last changes fastest.
Arguments:
- weights: bfloat16 [2, 24576, 6144], P(None, 'row', 'col'), may hold values from -0.15625 to 0.15625
- pattern: int32 [2, 192, 48], P(None, 'row', 'col'), may hold values 0 or 1
- sketch: bfloat16 [6144, 512], P('col'), may hold values from -6 to 6
Outputs:
- basis: float32 [2, 24576, 512], P(None, ('row', 'col'))
Inputs may be any that keep to these rules, and one draw needn't show every extreme that they name: `pattern`: 1 marks a block of the sparse part, 0 a block of the residual.
All inputs are finite; a program needn't handle non-finite values.
Results may differ from a plain program's by a relative error of at most 0.0003.
Values sent between devices are 32-bit elements; how exact they have to be, the bound alone decides.
No kernel may reach another device: no remote copies, remote signals or barrier semaphores. Data moves between devices by JAX's collectives and lax.ppermute only.
A program may use at most 64 MiB of HBM per device.

v0:
```python
import jax
import jax.numpy as jnp
from jax import lax
from jax.sharding import PartitionSpec as P

M = 24576
BLOCK = 128
LAYERS = 2


def make_basis(rows_here, gram):
    lower = jnp.linalg.cholesky(gram)
    solved = lax.linalg.triangular_solve(
        lower, rows_here, left_side=False, lower=True, transpose_a=True
    )
    return solved * jnp.sqrt(jnp.float32(M))


def local_gram(rows_here):
    return lax.dot_general(
        rows_here,
        rows_here,
        (((0,), (0,)), ((), ())),
        precision=lax.Precision.HIGHEST,
        preferred_element_type=jnp.float32,
    )


def body(weights, pattern, sketch):
    row_count = weights.shape[1]
    col_count = weights.shape[2]
    outputs = []
    for layer in range(LAYERS):
        keep = (1 - pattern[layer]).astype(jnp.bfloat16)
        shaped = (
            weights[layer].reshape(row_count // BLOCK, BLOCK, col_count // BLOCK, BLOCK)
            * keep[:, None, :, None]
        )
        leftover = shaped.reshape(row_count, col_count)
        rows_here = lax.psum_scatter(
            jnp.dot(leftover, sketch, preferred_element_type=jnp.float32),
            "col",
            scatter_dimension=0,
            tiled=True,
        )
        sampled = lax.all_gather(rows_here, "col", axis=0, tiled=True)
        gram = lax.psum(local_gram(sampled), "row") / M
        outputs.append(make_basis(rows_here, gram))
    return jnp.stack(outputs, axis=0)


def solution(mesh):
    return jax.shard_map(
        body,
        mesh=mesh,
        in_specs=(P(None, "row", "col"), P(None, "row", "col"), P("col", None)),
        out_specs=P(None, ("row", "col"), None),
        check_vma=False,
    )
```

profile of v0, /device:TPU:1, one launch (start us, length us, event | category | flops | bytes accessed | tf_op | source)
XLA Modules:
  0.0 823.3 jit_solution(7290686633852218556)
XLA Ops:
  6.5 0.8 subtract_convert_fusion.1
  7.3 1.4 fusion.70
  9.1 1.8 fusion.4
  11.4 1.8 fusion.2
  13.3 91.7 %reduce-scatter.3.cloned.1.call-done = f32[48,512]{1,0:T(8,128)} async-done(((f32[768,512]{1,0:T(8,128)}), f32[48,512]{1,0:T(8,128)}) %reduce-scatter.3.cloned.1.call-update) | async-done | bytes 98320 | tf_op jit(solution)/shard_map/reduce_scatter | solution.py:40
  105.0 93.3 %reduce-scatter.5.cloned.1.call-done = f32[48,512]{1,0:T(8,128)} async-done(((f32[768,512]{1,0:T(8,128)}), f32[48,512]{1,0:T(8,128)}) %reduce-scatter.5.cloned.1.call-update) | async-done | bytes 98320 | tf_op jit(solution)/shard_map/reduce_scatter | solution.py:40
  198.4 61.8 %all-gather.3.cloned.1.call-done = f32[768,512]{1,0:T(8,128)} async-done(((f32[48,512]{1,0:T(8,128)}), f32[768,512]{1,0:T(8,128)}) %all-gather.3.cloned.1.call-update) | async-done | bytes 1572880 | tf_op jit(solution)/shard_map/all_gather | solution.py:46
  260.2 5.6 fusion.71
  265.8 55.8 %all-gather.5.cloned.1.call-done = f32[768,512]{1,0:T(8,128)} async-done(((f32[48,512]{1,0:T(8,128)}), f32[768,512]{1,0:T(8,128)}) %all-gather.5.cloned.1.call-update) | async-done | bytes 1572880 | tf_op jit(solution)/shard_map/all_gather | solution.py:46
  321.6 5.6 fusion.72
  327.2 217.0 %all-reduce.4.cloned.1.call-done = (f32[512,512]{0,1:T(8,128)}, f32[512,512]{0,1:T(8,128)}) async-done(((f32[512,512]{0,1:T(8,128)}, f32[512,512]{0,1:T(8,128)}), (f32[512,512]{0,1:T(8,128)}, f32[512,512]{0,1:T(8,128)})) %all-reduce.4.cloned.1.call-update) | async-done | bytes 2097168 | tf_op jit(solution)/shard_map/psum | solution.py:47
  544.2 1.3 broadcast_multiply_fusion.1
  545.6 0.3 copy.12
  545.9 0.9 copy-done.2
  547.1 11.7 %cholesky.286 = f32[128,128]{1,0:T(8,128)S(1)} custom-call(f32[128,128]{1,0:T(8,128)S(1)} %cholesky.426), custom_call_target="Cholesky" | custom-call | tf_op jit(solution)/shard_map/jit(cholesky)/cholesky | solution.py:12
  558.8 10.0 %custom-call.27 = f32[1,128,128]{1,2,0:T(8,128)S(1)} custom-call(f32[1,128,128]{2,1,0:T(8,128)S(1)} %get-tuple-element.56), custom_call_target="InvertDiagBlocksLowerTriangular" | custom-call | tf_op jit(solution)/shard_map/jit(cholesky)/cholesky | solution.py:12
  569.6 11.7 %cholesky.305 = f32[128,128]{1,0:T(8,128)S(1)} custom-call(f32[128,128]{1,0:T(8,128)S(1)} %cholesky.430), custom_call_target="Cholesky" | custom-call | tf_op jit(solution)/shard_map/jit(cholesky)/cholesky | solution.py:12
  581.4 0.6 compare_reduce_fusion.6
  582.0 0.7 compare_reduce_fusion.7
  582.7 9.8 %custom-call.28 = f32[1,128,128]{1,2,0:T(8,128)S(1)} custom-call(f32[1,128,128]{2,1,0:T(8,128)S(1)} %get-tuple-element.53), custom_call_target="InvertDiagBlocksLowerTriangular" | custom-call | tf_op jit(solution)/shard_map/jit(cholesky)/cholesky | solution.py:12
  592.8 0.4 convolution_subtract_fusion.3
  593.2 11.7 %cholesky.326 = f32[128,128]{1,0:T(8,128)S(1)} custom-call(f32[128,128]{1,0:T(8,128)S(1)} %cholesky.435), custom_call_target="Cholesky" | custom-call | tf_op jit(solution)/shard_map/jit(cholesky)/cholesky | solution.py:12
  605.0 0.7 compare_reduce_fusion.5
  605.6 10.2 %custom-call.29 = f32[1,128,128]{1,2,0:T(8,128)S(1)} custom-call(f32[1,128,128]{2,1,0:T(8,128)S(1)} %get-tuple-element.50), custom_call_target="InvertDiagBlocksLowerTriangular" | custom-call | tf_op jit(solution)/shard_map/jit(cholesky)/cholesky | solution.py:12
  616.0 0.4 convolution_subtract_fusion.5
  616.4 11.7 %cholesky.343 = f32[128,128]{1,0:T(8,128)S(1)} custom-call(f32[128,128]{1,0:T(8,128)S(1)} %convolution_subtract_fusion.5), custom_call_target="Cholesky" | custom-call | tf_op jit(solution)/shard_map/jit(cholesky)/cholesky | solution.py:12
  628.2 0.7 compare_reduce_fusion.4
  631.6 8.1 while.4
  631.7 0.6 fusion.91
  632.3 1.3 bitcast_dynamic-update-slice_fusion.4
  633.7 0.6 fusion.91
  634.3 1.3 bitcast_dynamic-update-slice_fusion.4
  635.7 0.6 fusion.91
  636.3 1.3 bitcast_dynamic-update-slice_fusion.4
  637.8 0.6 fusion.91
  638.4 1.3 bitcast_dynamic-update-slice_fusion.4
  639.7 39.5 %custom-call.30 = f32[4,128,128]{1,2,0:T(8,128)S(1)} custom-call(f32[4,128,128]{2,1,0:T(8,128)S(1)} %get-tuple-element.21), custom_call_target="InvertDiagBlocksLowerTriangular" | custom-call | tf_op jit(solution)/shard_map/triangular_solve/custom-call.3 | solution.py:13
  680.3 0.4 convolution_subtract_fusion.9
  680.8 0.7 fusion.24
  682.2 11.7 %cholesky.358 = f32[128,128]{1,0:T(8,128)S(1)} custom-call(f32[128,128]{1,0:T(8,128)S(1)} %cholesky.439), custom_call_target="Cholesky" | custom-call | tf_op jit(solution)/shard_map/jit(cholesky)/cholesky | solution.py:12
  693.9 9.8 %custom-call.31 = f32[1,128,128]{1,2,0:T(8,128)S(1)} custom-call(f32[1,128,128]{2,1,0:T(8,128)S(1)} %get-tuple-element.66), custom_call_target="InvertDiagBlocksLowerTriangular" | custom-call | tf_op jit(solution)/shard_map/jit(cholesky)/cholesky | solution.py:12
  704.5 11.7 %cholesky.377 = f32[128,128]{1,0:T(8,128)S(1)} custom-call(f32[128,128]{1,0:T(8,128)S(1)} %cholesky.443), custom_call_target="Cholesky" | custom-call | tf_op jit(solution)/shard_map/jit(cholesky)/cholesky | solution.py:12
  716.3 0.6 compare_reduce_fusion.2
  716.9 0.7 compare_reduce_fusion.3
  717.6 10.0 %custom-call.32 = f32[1,128,128]{1,2,0:T(8,128)S(1)} custom-call(f32[1,128,128]{2,1,0:T(8,128)S(1)} %get-tuple-element.63), custom_call_target="InvertDiagBlocksLowerTriangular" | custom-call | tf_op jit(solution)/shard_map/jit(cholesky)/cholesky | solution.py:12
  727.9 0.4 convolution_subtract_fusion.2
  728.3 11.7 %cholesky.398 = f32[128,128]{1,0:T(8,128)S(1)} custom-call(f32[128,128]{1,0:T(8,128)S(1)} %cholesky.448), custom_call_target="Cholesky" | custom-call | tf_op jit(solution)/shard_map/jit(cholesky)/cholesky | solution.py:12
  740.1 0.7 compare_reduce_fusion.1
  740.7 9.8 %custom-call.33 = f32[1,128,128]{1,2,0:T(8,128)S(1)} custom-call(f32[1,128,128]{2,1,0:T(8,128)S(1)} %get-tuple-element.60), custom_call_target="InvertDiagBlocksLowerTriangular" | custom-call | tf_op jit(solution)/shard_map/jit(cholesky)/cholesky | solution.py:12
  750.8 0.4 convolution_subtract_fusion.4
  751.1 12.0 %cholesky.415 = f32[128,128]{1,0:T(8,128)S(1)} custom-call(f32[128,128]{1,0:T(8,128)S(1)} %convolution_subtract_fusion.4), custom_call_target="Cholesky" | custom-call | tf_op jit(solution)/shard_map/jit(cholesky)/cholesky | solution.py:12
  763.1 0.7 compare_reduce_fusion
  766.5 8.1 while.5
  766.6 0.6 fusion.92
  767.2 1.3 bitcast_dynamic-update-slice_fusion.5
  768.7 0.6 fusion.92
  769.3 1.3 bitcast_dynamic-update-slice_fusion.5
  770.7 0.6 fusion.92
  771.3 1.3 bitcast_dynamic-update-slice_fusion.5
  772.7 0.6 fusion.92
  773.3 1.3 bitcast_dynamic-update-slice_fusion.5
  774.7 39.3 %custom-call.34 = f32[4,128,128]{1,2,0:T(8,128)S(1)} custom-call(f32[4,128,128]{2,1,0:T(8,128)S(1)} %get-tuple-element.22), custom_call_target="InvertDiagBlocksLowerTriangular" | custom-call | tf_op jit(solution)/shard_map/triangular_solve/custom-call.3 | solution.py:13
  815.1 0.4 convolution_subtract_fusion.6
  815.6 0.7 pad_maximum_fusion
  (81 shorter events, 8.1 us)
Async XLA Ops:
  6.5 2.6 copy-start
  6.5 98.4 %reduce-scatter.3.cloned.1.call-start = ((), (), s32[]{:S(2)}) async-start(), calls=%async_computation.2 | async-start | bytes 1671168 | tf_op jit(solution)/shard_map/reduce_scatter | solution.py:40
  10.9 187.4 %reduce-scatter.5.cloned.1.call-start = ((), (), s32[]{:S(2)}) async-start(), calls=%async_computation.4 | async-start | bytes 1671168 | tf_op jit(solution)/shard_map/reduce_scatter | solution.py:40
  13.2 247.0 %all-gather.3.cloned.1.call-start = ((), (), s32[]{:S(2)}) async-start(), calls=%async_computation.3 | async-start | bytes 1671168 | tf_op jit(solution)/shard_map/all_gather | solution.py:46
  104.9 216.6 %all-gather.5.cloned.1.call-start = ((), (), s32[]{:S(2)}) async-start(), calls=%async_computation.5 | async-start | bytes 1671168 | tf_op jit(solution)/shard_map/all_gather | solution.py:46
  198.4 345.9 %all-reduce.4.cloned.1.call-start = ((), (), s32[]{:S(2)}) async-start(), calls=%async_computation.6 | async-start | bytes 4194304 | tf_op jit(solution)/shard_map/psum | solution.py:47
  545.6 1.2 copy-start.2
  631.4 47.8 %copy-start.4 = (f32[48,512]{1,0:T(8,128)S(1)}, f32[48,512]{1,0:T(8,128)}, u32[]{:S(2)}) copy-start(f32[48,512]{1,0:T(8,128)} %reduce-scatter.3.cloned.1.call-done) | copy-start | bytes 294916
  631.5 49.9 %copy-start.1 = (f32[512,512]{0,1:T(8,128)S(1)}, f32[512,512]{0,1:T(8,128)}, u32[]{:S(2)}) copy-start(f32[512,512]{0,1:T(8,128)} %get-tuple-element.39) | copy-start | bytes 3145732
  766.4 47.7 %copy-start.3 = (f32[48,512]{1,0:T(8,128)S(1)}, f32[48,512]{1,0:T(8,128)}, u32[]{:S(2)}) copy-start(f32[48,512]{1,0:T(8,128)} %reduce-scatter.5.cloned.1.call-done) | copy-start | bytes 294916
  766.5 49.1 %copy-start.5 = (f32[1,48,512]{2,1,0:T(8,128)S(1)}, f32[1,48,512]{2,1,0:T(8,128)}, u32[]{:S(2)}) copy-start(f32[1,48,512]{2,1,0:T(8,128)} %fusion.24) | copy-start | bytes 294916
Sparse Core Ops, SparseCore 0:
  11.4 93.4 reduce-scatter.2
  109.0 89.2 reduce-scatter.4
  201.4 58.8 all-gather.2
  263.1 58.4 all-gather.4
  327.3 216.8 all-reduce.3
where the time goes:
time: 833 us; the launch traced here: 823 us
  waiting for transfers between devices  520 us (62%)
  other arithmetic  242 us (29%)
  matrix products  21.5 us (3%)
  local copies, waits for them, and re-layouts  20.2 us (2%)
  between operations  19.1 us (2%)
    psum x1, waiting for transfers between devices, body(): gram = lax.psum(local_gram(sampled), 'row') / M  217 us
    reduce_scatter x2, waiting for transfers between devices, body(): lax.psum_scatter(jnp.dot(leftover, sketch, preferred_element_type=jnp.flo...  185 us
    another operation x30, other arithmetic, make_basis(): lower = jnp.linalg.cholesky(gram)  159 us
    all_gather x2, waiting for transfers between devices, body(): sampled = lax.all_gather(rows_here, 'col', axis=0, tiled=True)  118 us
    another operation x5, other arithmetic, make_basis(): lax.linalg.triangular_solve(lower, rows_here, left_side=False, lower=True...  79.1 us
  transfers between devices with their start and end apart: 5, of which 5 were waited for; matrix products, arithmetic and copies ran while one was open for 1% of the time, Pallas kernels for 0%

commit v1 on v0

v1 whole, which is shorter than its diff:
```python
import jax
import jax.numpy as jnp
from jax import lax
from jax.experimental import pallas as pl
from jax.experimental.pallas import tpu as pltpu
from jax.sharding import PartitionSpec as P

M = 24576
BLOCK = 128
LAYERS = 2
SUP = 32
PAN = 8
HI = lax.Precision.HIGHEST


def nt(a, b):
    return lax.dot_general(a, b, (((1,), (1,)), ((), ())), precision=HI, preferred_element_type=jnp.float32)
def tn(a, b):
    return lax.dot_general(a, b, (((0,), (0,)), ((), ())), precision=HI, preferred_element_type=jnp.float32)

def inverse_factor(x_ref):
    lane8 = lax.broadcasted_iota(jnp.int32, (PAN, BLOCK), 1)
    row8 = lax.broadcasted_iota(jnp.int32, (PAN, BLOCK), 0)
    for first in range(0, BLOCK, SUP):
        rows = [x_ref[first + PAN * i : first + PAN * (i + 1), :] for i in range(SUP // PAN)]
        for p in range(SUP // PAN):
            lead = first + PAN * p
            cols = [[jnp.broadcast_to(rows[i][:, lead + k : lead + k + 1], (PAN, BLOCK)) for k in range(PAN)] for i in range(p, SUP // PAN)]
            diag = jnp.ones((PAN, BLOCK), jnp.float32)
            for k in range(PAN):
                pivot = jnp.broadcast_to(cols[0][k][k : k + 1, :], (PAN, BLOCK))
                inv = 1.0 / pivot
                diag = jnp.where(row8 == k, pivot, diag)
                source = jnp.where(lane8 == lead + k, 1.0, jnp.broadcast_to(rows[p][k : k + 1, :], (PAN, BLOCK)))
                heads = [jnp.broadcast_to(cols[0][m][k : k + 1, :], (PAN, BLOCK)) * inv for m in range(k + 1, PAN)]
                for i in range(p, SUP // PAN):
                    col = cols[i - p][k]
                    if i == p:
                        col = jnp.where(row8 > k, col, 0.0)
                        keep = jnp.where((lane8 == lead + k) & (row8 > k), 0.0, rows[i])
                        keep = jnp.where((lane8 == lead + k) & (row8 == k), 1.0, keep)
                    else:
                        keep = jnp.where(lane8 == lead + k, 0.0, rows[i])
                    rows[i] = keep - (col * inv) * source
                    for m in range(k + 1, PAN):
                        cols[i - p][m] = cols[i - p][m] - col * heads[m - k - 1]
            rows[p] = rows[p] * lax.rsqrt(diag)
        whole = jnp.concatenate(rows, axis=0)
        lane = lax.broadcasted_iota(jnp.int32, (SUP, BLOCK), 1)
        row = lax.broadcasted_iota(jnp.int32, (SUP, BLOCK), 0) + first
        low = jnp.where((lane > row) & (lane < first + SUP), 0.0, whole)
        last = first + SUP
        if last < BLOCK:
            x_ref[first:last, :] = jnp.where(lane > row, 0.0, whole)
            delta = tn(whole, low)
            lane_b = lax.broadcasted_iota(jnp.int32, (BLOCK - last, BLOCK), 1)
            below = x_ref[last:BLOCK, :]
            below = jnp.where((lane_b >= first) & (lane_b < last), 0.0, below)
            x_ref[last:BLOCK, :] = below - delta[last:BLOCK, :]
        else:
            x_ref[first:last, :] = low
    return x_ref[...]

def start_of(n, j):
    return BLOCK * sum(n - i for i in range(j))

def basis_kernel(gram_ref, rows_ref, out_ref, a_ref, s_ref, x_ref):
    n = rows_ref.shape[1] // BLOCK
    a_ref[...] = gram_ref[...]
    s_ref[...] = rows_ref[...]
    for k in range(n):
        base = start_of(n, k)
        x_ref[...] = a_ref[base : base + BLOCK, :]
        w = inverse_factor(x_ref)
        tail = s_ref[:, k * BLOCK : (k + 1) * BLOCK]
        below = (n - 1 - k) * BLOCK
        if below:
            stacked = jnp.concatenate([a_ref[base + BLOCK : base + BLOCK + below, :], tail], axis=0)
        else:
            stacked = tail
        panel = nt(stacked, w)
        out_ref[:, k * BLOCK : (k + 1) * BLOCK] = panel[below:, :] * float(M)
        for j in range(k + 1, n):
            off = (j - k - 1) * BLOCK
            update = nt(panel[off:, :], panel[off : off + BLOCK, :])
            height = (n - j) * BLOCK
            to = start_of(n, j)
            a_ref[to : to + height, :] = a_ref[to : to + height, :] - update[:height, :]
            s_ref[:, j * BLOCK : (j + 1) * BLOCK] = s_ref[:, j * BLOCK : (j + 1) * BLOCK] - update[height:, :]

def basis(gram, rows):
    return pl.pallas_call(
        basis_kernel,
        out_shape=jax.ShapeDtypeStruct(rows.shape, jnp.float32),
        in_specs=[vmem(), vmem()],
        out_specs=vmem(),
        scratch_shapes=[pltpu.VMEM(gram.shape, jnp.float32), pltpu.VMEM(rows.shape, jnp.float32), pltpu.VMEM((BLOCK, BLOCK), jnp.float32)],
        name="basis",
    )(gram, rows)


def vmem():
    return pl.BlockSpec(memory_space=pltpu.VMEM)


def product_kernel(pattern_ref, weights_ref, sketch_ref, out_ref):
    layer = pl.program_id(0)
    height, width = weights_ref.shape[1:]
    strips = []
    for i in range(height // BLOCK):
        parts = []
        for j in range(width // BLOCK):
            block = weights_ref[0, i * BLOCK : (i + 1) * BLOCK, j * BLOCK : (j + 1) * BLOCK]
            parts.append(jnp.where(pattern_ref[layer, i, j] == 1, jnp.zeros_like(block), block))
        strips.append(jnp.concatenate(parts, axis=1))
    leftover = jnp.concatenate(strips, axis=0)
    product = jnp.dot(leftover, sketch_ref[...], preferred_element_type=jnp.float32)
    out_ref[...] = product.reshape(out_ref.shape)


def product(weights, pattern, sketch, peers):
    layers, height, width = weights.shape
    rank = sketch.shape[1]
    share = height // peers
    return pl.pallas_call(
        product_kernel,
        grid=(layers,),
        out_shape=jax.ShapeDtypeStruct((peers, layers, share, rank), jnp.float32),
        in_specs=[
            pl.BlockSpec(memory_space=pltpu.SMEM),
            pl.BlockSpec((1, height, width), lambda l: (l, 0, 0)),
            pl.BlockSpec((width, rank), lambda l: (0, 0)),
        ],
        out_specs=pl.BlockSpec((peers, 1, share, rank), lambda l: (0, l, 0, 0)),
        name="product",
    )(pattern, weights, sketch)


def gram_kernel(mine_ref, got_ref, gram_ref, rows_ref):
    rows = jnp.concatenate([mine_ref[...], got_ref[...]], axis=0)
    rows_ref[...] = rows
    n = rows.shape[1] // BLOCK
    for j in range(n):
        to = start_of(n, j)
        gram_ref[to : to + (n - j) * BLOCK, :] = tn(rows[:, j * BLOCK :], rows[:, j * BLOCK : (j + 1) * BLOCK])


def local_gram(mine, got):
    share, rank = mine.shape
    n = rank // BLOCK
    return pl.pallas_call(
        gram_kernel,
        out_shape=(
            jax.ShapeDtypeStruct((start_of(n, n), BLOCK), jnp.float32),
            jax.ShapeDtypeStruct((2 * share, rank), jnp.float32),
        ),
        in_specs=[vmem(), vmem()],
        out_specs=(vmem(), vmem()),
        name="local_gram",
    )(mine, got)


def make_body(row_size, peers):
    chips = row_size // 2
    cores = [(2 * z + c, 2 * z + 1 - c) for z in range(chips) for c in range(2)]
    groups = [[2 * z + c for z in range(chips)] for c in range(2)]

    def to_col(x):
        return lax.all_to_all(x, "col", 0, 0)

    def to_chips(x):
        return lax.all_to_all(x, "row", 0, 0, axis_index_groups=groups)

    def summed_gram(gram):
        height = gram.shape[0] // peers
        piece = jnp.sum(to_col(gram.reshape(peers, height, BLOCK)), axis=0)
        part = jnp.sum(to_chips(piece.reshape(chips, height // chips, BLOCK)), axis=0)
        piece = to_chips(jnp.broadcast_to(part, (chips, *part.shape))).reshape(height, BLOCK)
        return to_col(jnp.broadcast_to(piece, (peers, *piece.shape))).reshape(gram.shape)

    def body(weights, pattern, sketch):
        second = (lax.axis_index("row") % 2) == 1
        partial = product(weights, pattern, sketch, peers)
        sampled = jnp.sum(to_col(partial), axis=0)
        mine = jnp.where(second, sampled[1], sampled[0])
        other = jnp.where(second, sampled[0], sampled[1])
        got = lax.ppermute(other, "row", cores)
        gram, rows = local_gram(mine, got)
        out = basis(summed_gram(gram), rows)
        share = mine.shape[0]
        own, away = out[:share], out[share:]
        back = lax.ppermute(away, "row", cores)
        return jnp.stack([jnp.where(second, back, own), jnp.where(second, own, back)], axis=0)

    return body


def solution(mesh):
    return jax.shard_map(
        make_body(mesh.shape["row"], mesh.shape["col"]),
        mesh=mesh,
        in_specs=(P(None, "row", "col"), P(None, "row", "col"), P("col", None)),
        out_specs=P(None, ("row", "col"), None),
        check_vma=False,
    )
```

time: 833 us -> 170 us (0.20); the launches traced: 823 us -> 169 us
  waiting for transfers between devices: 520 us -> 41.9 us
  other arithmetic: 242 us -> 2.61 us
  blocking collectives: 0 us -> 74.3 us
  Pallas kernels: 0 us -> 26.3 us
  matrix products: 21.5 us -> 0 us
  starting transfers between devices: 0.16 us -> 21.1 us
  between operations: 19.1 us -> 0.07 us
  local copies, waits for them, and re-layouts: 20.2 us -> 2.96 us
    another operation x38 -> x2, other arithmetic: 240 us -> 1.6 us  [body(): jnp.stack([jnp.where(second, back, own), jnp.where(second, own, back)], a...]
    psum x1 -> x0, waiting for transfers between devices: 217 us -> none  [body(): gram = lax.psum(local_gram(sampled), 'row') / M]
    reduce_scatter x2 -> x0, waiting for transfers between devices: 185 us -> none  [body(): lax.psum_scatter(jnp.dot(leftover, sketch, preferred_element_type=jnp.flo...]
    all_gather x2 -> x0, waiting for transfers between devices: 118 us -> none  [body(): sampled = lax.all_gather(rows_here, 'col', axis=0, tiled=True)]
    all_to_all x0 -> x4, blocking collectives: none -> 74.3 us  [the longest x2 45.1 us: to_chips(): return lax.all_to_all(x, 'row', 0, 0, axis_index_groups=groups)]
    all_to_all x0 -> x1, waiting for transfers between devices: none -> 40.1 us  [to_col(): return lax.all_to_all(x, 'col', 0, 0)]
    pallas_call x0 -> x3, Pallas kernels: none -> 26.3 us  [the longest x1 20.3 us: basis(): pl.pallas_call(basis_kernel, out_shape=jax.ShapeDtypeStruct(rows.shape, j...]
    another operation x35 -> x0, local copies, waits for them, and re-layouts: 16.4 us -> none  [the longest x27 16.2 us: make_basis(): lax.linalg.triangular_solve(lower, rows_here, left_side=False, lower=True...]
  transfers between devices with their start and end apart: 5 -> 3, of which waited for: 5 -> 3; matrix products, arithmetic and copies ran while one was open for 1% -> 0% of each run, Pallas kernels for 0% -> 0%
where the time goes in v1:
time: 170 us; the launch traced here: 169 us
  blocking collectives  74.3 us (44%)
  waiting for transfers between devices  41.9 us (25%)
  Pallas kernels  26.3 us (15%)
  starting transfers between devices  21.1 us (12%)
  local copies, waits for them, and re-layouts  2.96 us (2%)
  other arithmetic  2.61 us (2%)
    all_to_all x2, blocking collectives, to_chips(): return lax.all_to_all(x, 'row', 0, 0, axis_index_groups=groups)  45.1 us
    all_to_all x1, waiting for transfers between devices, to_col(): return lax.all_to_all(x, 'col', 0, 0)  40.1 us
    all_to_all x2, blocking collectives, to_col(): return lax.all_to_all(x, 'col', 0, 0)  29.2 us
    pallas_call x1, Pallas kernels, basis(): pl.pallas_call(basis_kernel, out_shape=jax.ShapeDtypeStruct(rows.shape, j...  20.3 us
    all_to_all x1, starting transfers between devices, to_col(): return lax.all_to_all(x, 'col', 0, 0)  7.56 us
    ppermute x1, starting transfers between devices, body(): back = lax.ppermute(away, 'row', cores)  7.13 us
    ppermute x1, starting transfers between devices, body(): got = lax.ppermute(other, 'row', cores)  6.4 us
    pallas_call x1, Pallas kernels, product(): pl.pallas_call(product_kernel, grid=(layers,), out_shape=jax.ShapeDtypeSt...  3.52 us
  transfers between devices with their start and end apart: 3, of which 3 were waited for; matrix products, arithmetic and copies ran while one was open for 0% of the time, Pallas kernels for 0%

profile of v1, /device:TPU:1, one launch (start us, length us, event | category | flops | bytes accessed | tf_op | source)
XLA Modules:
  0.0 169.2 jit_solution(15415402602695367934)
XLA Ops:
  0.0 1.4 copy.5.pattern_ref
  1.4 3.5 %product.1 = f32[16,2,48,512]{3,2,1,0:T(8,128)} custom-call(s32[2,6,3]{2,1,0:T(8,128)} %copy.5.pattern_ref, bf16[2,768,384]{2,1,0:T(8,128)(2,1)} %weights_ref.1, bf16[384,512]{1,0:T(8,128)(2,1)} %sketch_ref.1), custom_call_target="tpu_custom_call" | custom-call | tf_op jit(solution)/shard_map/product/pallas_call | solution.py:125
  4.9 7.6 %all-to-all-start = ((f32[16,2,48,512]{3,2,1,0:T(8,128)}), f32[16,2,48,512]{3,2,1,0:T(8,128)S(1)}, u32[]{:S(2)}, u32[]{:S(2)}) async-start(f32[16,2,48,512]{3,2,1,0:T(8,128)} %product.1), calls=%async_computation | async-start | bytes 6291456 | tf_op jit(solution)/shard_map/all_to_all | solution.py:169
  12.5 40.1 %all-to-all-done = f32[16,2,48,512]{3,2,1,0:T(8,128)S(1)} async-done(((f32[16,2,48,512]{3,2,1,0:T(8,128)}), f32[16,2,48,512]{3,2,1,0:T(8,128)S(1)}, u32[]{:S(2)}, u32[]{:S(2)}) %all-to-all-start) | async-done | bytes 3145760 | tf_op jit(solution)/shard_map/all_to_all | solution.py:169
  52.6 0.3 reduce_sum.27
  52.9 0.7 select_bitcast_fusion.2
  53.5 6.4 %collective-permute-start = (f32[48,512]{1,0:T(8,128)S(1)}, f32[48,512]{1,0:T(8,128)S(1)}, u32[]{:S(2)}, u32[]{:S(2)}) collective-permute-start(f32[48,512]{1,0:T(8,128)S(1)} %get-tuple-element.11), channel_id=1, source_target_pairs={{0,16},{16,0},{32,48},{48,32},{64,80},{80,64},{96,112},{112,96},{1... | collective-permute-start | bytes 294920 | tf_op jit(solution)/shard_map/ppermute | solution.py:187
  59.9 0.9 collective-permute-done.got_ref
  60.8 0.0 copy-start
  60.8 0.6 copy-done
  61.5 2.5 %local_gram.1 = (f32[1280,128]{1,0:T(8,128)}, f32[96,512]{1,0:T(8,128)}) custom-call(f32[48,512]{1,0:T(8,128)} %get-tuple-element.12.mine_ref, f32[48,512]{1,0:T(8,128)} %copy-done), custom_call_target="tpu_custom_call" | custom-call | tf_op jit(solution)/shard_map/local_gram/pallas_call | solution.py:151
  64.0 16.1 %all_to_all.25 = f32[16,80,128]{2,1,0:T(8,128)S(1)} all-to-all(f32[16,80,128]{2,1,0:T(8,128)} %bitcast.11), channel_id=1, replica_groups=mesh['row'=32,'col'=16] {'col'}, dimensions={0} | all-to-all | bytes 1310720 | tf_op jit(solution)/shard_map/all_to_all | solution.py:169
  80.1 30.7 %all_to_all.26 = f32[16,5,128]{2,1,0:T(8,128)S(1)} all-to-all(f32[16,5,128]{2,1,0:T(8,128)S(1)} %reshape.17), channel_id=1, replica_groups={{0,32,64,96,128,160,192,224,256,288,320,352,384,416,448,480},{16,48,80,..., dimensions={0} | all-to-all | bytes 81920 | tf_op jit(solution)/shard_map/all_to_all | solution.py:172
  110.9 14.4 %all_to_all.27 = f32[16,5,128]{2,1,0:T(8,128)S(1)} all-to-all(f32[16,5,128]{2,1,0:T(8,128)S(1)} %broadcast_in_dim.6), channel_id=1, replica_groups={{0,32,64,96,128,160,192,224,256,288,320,352,384,416,448,480},{16,48,80,..., dimensions={0} | all-to-all | bytes 81920 | tf_op jit(solution)/shard_map/all_to_all | solution.py:172
  125.3 13.1 %all_to_all.28 = f32[16,80,128]{2,1,0:T(8,128)} all-to-all(f32[16,80,128]{2,1,0:T(8,128)S(1)} %broadcast_in_dim.7), channel_id=1, replica_groups=mesh['row'=32,'col'=16] {'col'}, dimensions={0} | all-to-all | bytes 1310720 | tf_op jit(solution)/shard_map/all_to_all | solution.py:169
  138.4 20.3 %basis.1 = f32[96,512]{1,0:T(8,128)} custom-call(f32[1280,128]{1,0:T(8,128)} %bitcast.10, f32[96,512]{1,0:T(8,128)} %get-tuple-element.8.rows_ref), custom_call_target="tpu_custom_call" | custom-call | tf_op jit(solution)/shard_map/basis/pallas_call | solution.py:92
  158.7 0.9 slice.20
  159.6 7.1 %collective-permute-start.1 = (f32[48,512]{1,0:T(8,128)S(1)}, f32[48,512]{1,0:T(8,128)S(1)}, u32[]{:S(2)}, u32[]{:S(2)}) collective-permute-start(f32[48,512]{1,0:T(8,128)S(1)} %slice.20), channel_id=1, source_target_pairs={{0,16},{16,0},{32,48},{48,32},{64,80},{80,64},{96,112},{112,96},{1... | collective-permute-start | bytes 294920 | tf_op jit(solution)/shard_map/ppermute | solution.py:192
  166.7 0.9 collective-permute-done.1
  167.6 0.9 select_bitcast_fusion.1
  168.5 0.7 pad_maximum_fusion
  (6 shorter events, 0.1 us)
Async XLA Ops:
  4.9 47.7 %all-to-all-start = ((f32[16,2,48,512]{3,2,1,0:T(8,128)}), f32[16,2,48,512]{3,2,1,0:T(8,128)S(1)}, u32[]{:S(2)}, u32[]{:S(2)}) async-start(f32[16,2,48,512]{3,2,1,0:T(8,128)} %product.1), calls=%async_computation | async-start | bytes 6291456 | tf_op jit(solution)/shard_map/all_to_all | solution.py:169
  53.5 7.3 %collective-permute-start = (f32[48,512]{1,0:T(8,128)S(1)}, f32[48,512]{1,0:T(8,128)S(1)}, u32[]{:S(2)}, u32[]{:S(2)}) collective-permute-start(f32[48,512]{1,0:T(8,128)S(1)} %get-tuple-element.11), channel_id=1, source_target_pairs={{0,16},{16,0},{32,48},{48,32},{64,80},{80,64},{96,112},{112,96},{1... | collective-permute-start | bytes 294920 | tf_op jit(solution)/shard_map/ppermute | solution.py:187
  60.8 0.6 copy-start
  159.6 8.1 %collective-permute-start.1 = (f32[48,512]{1,0:T(8,128)S(1)}, f32[48,512]{1,0:T(8,128)S(1)}, u32[]{:S(2)}, u32[]{:S(2)}) collective-permute-start(f32[48,512]{1,0:T(8,128)S(1)} %slice.20), channel_id=1, source_target_pairs={{0,16},{16,0},{32,48},{48,32},{64,80},{80,64},{96,112},{112,96},{1... | collective-permute-start | bytes 294920 | tf_op jit(solution)/shard_map/ppermute | solution.py:192

commit v2 on v1

--- a/solution.py
+++ b/solution.py
@@ -10,6 +10,7 @@
 LAYERS = 2
 SUP = 32
 PAN = 8
+GRANT = 24 << 20
 HI = lax.Precision.HIGHEST
 
 
@@ -64,7 +65,7 @@
 def start_of(n, j):
     return BLOCK * sum(n - i for i in range(j))
 
-def basis_kernel(gram_ref, rows_ref, out_ref, a_ref, s_ref, x_ref):
+def basis_kernel(gram_ref, rows_ref, own_ref, away_ref, a_ref, s_ref, x_ref):
     n = rows_ref.shape[1] // BLOCK
     a_ref[...] = gram_ref[...]
     s_ref[...] = rows_ref[...]
@@ -79,7 +80,10 @@
         else:
             stacked = tail
         panel = nt(stacked, w)
-        out_ref[:, k * BLOCK : (k + 1) * BLOCK] = panel[below:, :] * float(M)
+        solved = panel[below:, :] * float(M)
+        share = solved.shape[0] // 2
+        own_ref[:, k * BLOCK : (k + 1) * BLOCK] = solved[:share, :]
+        away_ref[:, k * BLOCK : (k + 1) * BLOCK] = solved[share:, :]
         for j in range(k + 1, n):
             off = (j - k - 1) * BLOCK
             update = nt(panel[off:, :], panel[off : off + BLOCK, :])
@@ -91,9 +95,10 @@
 def basis(gram, rows):
     return pl.pallas_call(
         basis_kernel,
-        out_shape=jax.ShapeDtypeStruct(rows.shape, jnp.float32),
+        out_shape=(in_vmem((rows.shape[0] // 2, rows.shape[1])),) * 2,
         in_specs=[vmem(), vmem()],
-        out_specs=vmem(),
+        out_specs=(vmem(), vmem()),
+        compiler_params=pltpu.CompilerParams(vmem_limit_bytes=GRANT),
         scratch_shapes=[pltpu.VMEM(gram.shape, jnp.float32), pltpu.VMEM(rows.shape, jnp.float32), pltpu.VMEM((BLOCK, BLOCK), jnp.float32)],
         name="basis",
     )(gram, rows)
@@ -103,37 +108,80 @@
     return pl.BlockSpec(memory_space=pltpu.VMEM)
 
 
+def in_vmem(shape):
+    return pltpu.VMEM(shape, jnp.float32)
+
+
+def held(x):
+    return pltpu.with_memory_space_constraint(x, pltpu.VMEM)
+
+
 def product_kernel(pattern_ref, weights_ref, sketch_ref, out_ref):
-    layer = pl.program_id(0)
-    height, width = weights_ref.shape[1:]
-    strips = []
-    for i in range(height // BLOCK):
-        parts = []
-        for j in range(width // BLOCK):
-            block = weights_ref[0, i * BLOCK : (i + 1) * BLOCK, j * BLOCK : (j + 1) * BLOCK]
-            parts.append(jnp.where(pattern_ref[layer, i, j] == 1, jnp.zeros_like(block), block))
-        strips.append(jnp.concatenate(parts, axis=1))
-    leftover = jnp.concatenate(strips, axis=0)
-    product = jnp.dot(leftover, sketch_ref[...], preferred_element_type=jnp.float32)
-    out_ref[...] = product.reshape(out_ref.shape)
+    layers, height, width = weights_ref.shape
+    peers, _, share, rank = out_ref.shape
+    for layer in range(layers):
+        strips = []
+        for i in range(height // BLOCK):
+            parts = []
+            for j in range(width // BLOCK):
+                block = weights_ref[layer, i * BLOCK : (i + 1) * BLOCK, j * BLOCK : (j + 1) * BLOCK]
+                parts.append(jnp.where(pattern_ref[j, layer, i] == 1, jnp.zeros_like(block), block))
+            strips.append(jnp.concatenate(parts, axis=1))
+        leftover = jnp.concatenate(strips, axis=0)
+        product = jnp.dot(leftover, sketch_ref[...], preferred_element_type=jnp.float32)
+        out_ref[:, layer] = product.reshape(peers, share, rank)
 
 
 def product(weights, pattern, sketch, peers):
     layers, height, width = weights.shape
     rank = sketch.shape[1]
-    share = height // peers
     return pl.pallas_call(
         product_kernel,
-        grid=(layers,),
-        out_shape=jax.ShapeDtypeStruct((peers, layers, share, rank), jnp.float32),
-        in_specs=[
-            pl.BlockSpec(memory_space=pltpu.SMEM),
-            pl.BlockSpec((1, height, width), lambda l: (l, 0, 0)),
-            pl.BlockSpec((width, rank), lambda l: (0, 0)),
-        ],
-        out_specs=pl.BlockSpec((peers, 1, share, rank), lambda l: (0, l, 0, 0)),
+        out_shape=in_vmem((peers, layers, height // peers, rank)),
+        in_specs=[pl.BlockSpec(memory_space=pltpu.SMEM), vmem(), vmem()],
+        out_specs=vmem(),
+        compiler_params=pltpu.CompilerParams(vmem_limit_bytes=GRANT),
         name="product",
     )(pattern, weights, sketch)
+
+
+def total_kernel(core_ref, parts_ref, mine_ref, other_ref):
+    core = core_ref[0]
+    peers = parts_ref.shape[0]
+    for layer, out_ref in ((core, mine_ref), (1 - core, other_ref)):
+        total = parts_ref[0, layer]
+        for peer in range(1, peers):
+            total = total + parts_ref[peer, layer]
+        out_ref[...] = total
+
+
+def total(core, parts):
+    shape = in_vmem(parts.shape[2:])
+    return pl.pallas_call(
+        total_kernel,
+        out_shape=(shape, shape),
+        in_specs=[pl.BlockSpec(memory_space=pltpu.SMEM), vmem()],
+        out_specs=(vmem(), vmem()),
+        compiler_params=pltpu.CompilerParams(vmem_limit_bytes=GRANT),
+        name="total",
+    )(core, held(parts))
+
+
+def merge_kernel(core_ref, own_ref, back_ref, out_ref):
+    core = core_ref[0]
+    out_ref[core] = own_ref[...]
+    out_ref[1 - core] = back_ref[...]
+
+
+def merge(core, own, back):
+    return pl.pallas_call(
+        merge_kernel,
+        out_shape=jax.ShapeDtypeStruct((LAYERS, *own.shape), jnp.float32),
+        in_specs=[pl.BlockSpec(memory_space=pltpu.SMEM), vmem(), vmem()],
+        out_specs=vmem(),
+        compiler_params=pltpu.CompilerParams(vmem_limit_bytes=GRANT),
+        name="merge",
+    )(core, held(own), held(back))
 
 
 def gram_kernel(mine_ref, got_ref, gram_ref, rows_ref):
@@ -151,13 +199,14 @@
     return pl.pallas_call(
         gram_kernel,
         out_shape=(
-            jax.ShapeDtypeStruct((start_of(n, n), BLOCK), jnp.float32),
-            jax.ShapeDtypeStruct((2 * share, rank), jnp.float32),
+            in_vmem((start_of(n, n), BLOCK)),
+            in_vmem((2 * share, rank)),
         ),
         in_specs=[vmem(), vmem()],
         out_specs=(vmem(), vmem()),
+        compiler_params=pltpu.CompilerParams(vmem_limit_bytes=GRANT),
         name="local_gram",
-    )(mine, got)
+    )(held(mine), held(got))
 
 
 def make_body(row_size, peers):
@@ -179,18 +228,14 @@
         return to_col(jnp.broadcast_to(piece, (peers, *piece.shape))).reshape(gram.shape)
 
     def body(weights, pattern, sketch):
-        second = (lax.axis_index("row") % 2) == 1
-        partial = product(weights, pattern, sketch, peers)
-        sampled = jnp.sum(to_col(partial), axis=0)
-        mine = jnp.where(second, sampled[1], sampled[0])
-        other = jnp.where(second, sampled[0], sampled[1])
+        core = (lax.axis_index("row") % 2).astype(jnp.int32).reshape(1)
+        pattern, core = lax.optimization_barrier((pattern.transpose(2, 0, 1), core))
+        mine, other = total(core, to_col(product(weights, pattern, sketch, peers)))
         got = lax.ppermute(other, "row", cores)
         gram, rows = local_gram(mine, got)
-        out = basis(summed_gram(gram), rows)
-        share = mine.shape[0]
-        own, away = out[:share], out[share:]
+        own, away = basis(held(summed_gram(gram)), held(rows))
         back = lax.ppermute(away, "row", cores)
-        return jnp.stack([jnp.where(second, back, own), jnp.where(second, own, back)], axis=0)
+        return merge(core, own, back)
 
     return body
 

time: 170 us -> 153 us (0.900)
  waiting for transfers between devices: 41.9 us -> 1.84 us
  blocking collectives: 74.3 us -> 114 us
  starting transfers between devices: 21.1 us -> 11.6 us
  Pallas kernels: 26.3 us -> 21.6 us
  other arithmetic: 2.61 us -> 0.06 us
    all_to_all x2 -> x3, blocking collectives: 29.2 us -> 74.4 us  [to_col(): return lax.all_to_all(x, 'col', 0, 0)]
    all_to_all x1 -> x0, waiting for transfers between devices: 40.1 us -> none  [to_col(): return lax.all_to_all(x, 'col', 0, 0)]
    all_to_all x1 -> x0, starting transfers between devices: 7.56 us -> none  [to_col(): return lax.all_to_all(x, 'col', 0, 0)]
    all_to_all x2, blocking collectives: 45.1 us -> 39.6 us  [to_chips(): return lax.all_to_all(x, 'row', 0, 0, axis_index_groups=groups)]
    pallas_call x3 -> x5, Pallas kernels: 26.3 us -> 21.6 us  [the longest x1 18.5 us: basis(): pl.pallas_call(basis_kernel, out_shape=(in_vmem((rows.shape[0] // 2, rows...]
    ppermute x1, starting transfers between devices: 6.4 us -> 4.55 us  [body(): got = lax.ppermute(other, 'row', cores)]
  transfers between devices with their start and end apart: 3 -> 2, of which waited for: 3 -> 2; matrix products, arithmetic and copies ran while one was open for 0% -> 0% of each run, Pallas kernels for 0% -> 0%
where the time goes in v2:
time: 153 us; the launch traced here: 152 us
  blocking collectives  114 us (75%)
  Pallas kernels  21.6 us (14%)
  starting transfers between devices  11.6 us (8%)
  local copies, waits for them, and re-layouts  3.02 us (2%)
  waiting for transfers between devices  1.84 us (1%)
    all_to_all x3, blocking collectives, to_col(): return lax.all_to_all(x, 'col', 0, 0)  74.4 us
    all_to_all x2, blocking collectives, to_chips(): return lax.all_to_all(x, 'row', 0, 0, axis_index_groups=groups)  39.6 us
    pallas_call x1, Pallas kernels, basis(): pl.pallas_call(basis_kernel, out_shape=(in_vmem((rows.shape[0] // 2, rows...  18.5 us
    ppermute x1, starting transfers between devices, body(): back = lax.ppermute(away, 'row', cores)  7.04 us
    ppermute x1, starting transfers between devices, body(): got = lax.ppermute(other, 'row', cores)  4.55 us
  transfers between devices with their start and end apart: 2, of which 2 were waited for; matrix products, arithmetic and copies ran while one was open for 0% of the time, Pallas kernels for 0%

profile of v2, /device:TPU:1, one launch (start us, length us, event | category | flops | bytes accessed | tf_op | source)
XLA Modules:
  0.0 152.2 jit_solution(3641139599351870403)
XLA Ops:
  0.0 0.0 copy-start
  0.0 1.3 copy-done
  1.3 0.0 copy-start.1
  1.3 1.0 copy-done.1
  2.3 0.0 copy-start.2
  2.3 0.7 copy-done.2
  3.0 1.6 %product.1 = f32[16,2,48,512]{3,2,1,0:T(8,128)S(1)} custom-call(s32[3,2,6]{2,1,0:T(2,128)S(1)} %bitcast.6, bf16[2,768,384]{2,1,0:T(8,128)(2,1)S(1)} %copy-done, bf16[384,512]{1,0:T(8,128)(2,1)S(1)} %copy-done.1), custom_call_target="tpu_custom_call" | custom-call | tf_op jit(solution)/shard_map/product/pallas_call | solution.py:138
  4.5 46.2 %all_to_all.25.parts_ref = f32[16,2,48,512]{3,2,1,0:T(8,128)S(1)} all-to-all(f32[16,2,48,512]{3,2,1,0:T(8,128)S(1)} %product.1), channel_id=1, replica_groups=mesh['row'=32,'col'=16] {'col'}, dimensions={0} | all-to-all | bytes 6291456 | tf_op jit(solution)/shard_map/all_to_all | solution.py:218
  50.7 0.1 total.1
  50.9 4.5 %collective-permute-start = (f32[48,512]{1,0:T(8,128)S(1)}, f32[48,512]{1,0:T(8,128)S(1)}, u32[]{:S(2)}, u32[]{:S(2)}) collective-permute-start(f32[48,512]{1,0:T(8,128)S(1)} %get-tuple-element.16), channel_id=1, source_target_pairs={{0,16},{16,0},{32,48},{48,32},{64,80},{80,64},{96,112},{112,96},{1... | collective-permute-start | bytes 294920 | tf_op jit(solution)/shard_map/ppermute | solution.py:234
  55.4 0.9 collective-permute-done.got_ref
  56.3 0.7 local_gram.1
  57.1 15.3 %all_to_all.26 = f32[16,80,128]{2,1,0:T(8,128)S(1)} all-to-all(f32[16,80,128]{2,1,0:T(8,128)S(1)} %bitcast.5), channel_id=1, replica_groups=mesh['row'=32,'col'=16] {'col'}, dimensions={0} | all-to-all | bytes 1310720 | tf_op jit(solution)/shard_map/all_to_all | solution.py:218
  72.4 25.2 %all_to_all.27 = f32[16,5,128]{2,1,0:T(8,128)S(1)} all-to-all(f32[16,5,128]{2,1,0:T(8,128)S(1)} %reshape.17), channel_id=1, replica_groups={{0,32,64,96,128,160,192,224,256,288,320,352,384,416,448,480},{16,48,80,..., dimensions={0} | all-to-all | bytes 81920 | tf_op jit(solution)/shard_map/all_to_all | solution.py:221
  97.7 14.4 %all_to_all.28 = f32[16,5,128]{2,1,0:T(8,128)S(1)} all-to-all(f32[16,5,128]{2,1,0:T(8,128)S(1)} %broadcast_in_dim.6), channel_id=1, replica_groups={{0,32,64,96,128,160,192,224,256,288,320,352,384,416,448,480},{16,48,80,..., dimensions={0} | all-to-all | bytes 81920 | tf_op jit(solution)/shard_map/all_to_all | solution.py:221
  112.1 12.9 %all_to_all.29 = f32[16,80,128]{2,1,0:T(8,128)S(1)} all-to-all(f32[16,80,128]{2,1,0:T(8,128)S(1)} %broadcast_in_dim.7), channel_id=1, replica_groups=mesh['row'=32,'col'=16] {'col'}, dimensions={0} | all-to-all | bytes 1310720 | tf_op jit(solution)/shard_map/all_to_all | solution.py:218
  125.1 18.5 %basis.1 = (f32[48,512]{1,0:T(8,128)S(1)}, f32[48,512]{1,0:T(8,128)S(1)}) custom-call(f32[1280,128]{1,0:T(8,128)S(1)} %bitcast.4, f32[96,512]{1,0:T(8,128)S(1)} %get-tuple-element.18.rows_ref), custom_call_target="tpu_custom_call" | custom-call | tf_op jit(solution)/shard_map/basis/pallas_call | solution.py:96
  143.5 7.0 %collective-permute-start.1 = (f32[48,512]{1,0:T(8,128)S(1)}, f32[48,512]{1,0:T(8,128)S(1)}, u32[]{:S(2)}, u32[]{:S(2)}) collective-permute-start(f32[48,512]{1,0:T(8,128)S(1)} %get-tuple-element.20), channel_id=1, source_target_pairs={{0,16},{16,0},{32,48},{48,32},{64,80},{80,64},{96,112},{112,96},{1... | collective-permute-start | bytes 294920 | tf_op jit(solution)/shard_map/ppermute | solution.py:237
  150.6 0.9 collective-permute-done.1.back_ref
  151.5 0.7 merge.1
  (6 shorter events, 0.1 us)
Async XLA Ops:
  0.0 1.3 copy-start
  1.3 1.0 copy-start.1
  2.3 0.7 copy-start.2
  50.9 5.5 %collective-permute-start = (f32[48,512]{1,0:T(8,128)S(1)}, f32[48,512]{1,0:T(8,128)S(1)}, u32[]{:S(2)}, u32[]{:S(2)}) collective-permute-start(f32[48,512]{1,0:T(8,128)S(1)} %get-tuple-element.16), channel_id=1, source_target_pairs={{0,16},{16,0},{32,48},{48,32},{64,80},{80,64},{96,112},{112,96},{1... | collective-permute-start | bytes 294920 | tf_op jit(solution)/shard_map/ppermute | solution.py:234
  143.5 8.0 %collective-permute-start.1 = (f32[48,512]{1,0:T(8,128)S(1)}, f32[48,512]{1,0:T(8,128)S(1)}, u32[]{:S(2)}, u32[]{:S(2)}) collective-permute-start(f32[48,512]{1,0:T(8,128)S(1)} %get-tuple-element.20), channel_id=1, source_target_pairs={{0,16},{16,0},{32,48},{48,32},{64,80},{80,64},{96,112},{112,96},{1... | collective-permute-start | bytes 294920 | tf_op jit(solution)/shard_map/ppermute | solution.py:237

commit v3 on v2

--- a/solution.py
+++ b/solution.py
@@ -1,3 +1,5 @@
+import math
+
 import jax
 import jax.numpy as jnp
 from jax import lax
@@ -212,20 +214,28 @@
 def make_body(row_size, peers):
     chips = row_size // 2
     cores = [(2 * z + c, 2 * z + 1 - c) for z in range(chips) for c in range(2)]
-    groups = [[2 * z + c for z in range(chips)] for c in range(2)]
+    near = math.isqrt(chips)
+    far = chips // near
+    near_groups = [[2 * (h * near + l) + c for l in range(near)] for h in range(far) for c in range(2)]
+    far_groups = [[2 * (h * near + l) + c for h in range(far)] for l in range(near) for c in range(2)]
 
     def to_col(x):
         return lax.all_to_all(x, "col", 0, 0)
 
-    def to_chips(x):
-        return lax.all_to_all(x, "row", 0, 0, axis_index_groups=groups)
+    def to_near(x):
+        return lax.all_to_all(x, "row", 0, 0, axis_index_groups=near_groups)
+
+    def to_far(x):
+        return lax.all_to_all(x, "row", 0, 0, axis_index_groups=far_groups)
+
+    def spread(x, exchange, count):
+        return exchange(jnp.broadcast_to(x, (count, *x.shape)))
 
     def summed_gram(gram):
-        height = gram.shape[0] // peers
-        piece = jnp.sum(to_col(gram.reshape(peers, height, BLOCK)), axis=0)
-        part = jnp.sum(to_chips(piece.reshape(chips, height // chips, BLOCK)), axis=0)
-        piece = to_chips(jnp.broadcast_to(part, (chips, *part.shape))).reshape(height, BLOCK)
-        return to_col(jnp.broadcast_to(piece, (peers, *piece.shape))).reshape(gram.shape)
+        piece = jnp.sum(to_col(gram.reshape(peers, gram.shape[0] // peers, BLOCK)), axis=0)
+        piece = jnp.sum(spread(piece, to_near, near), axis=0)
+        piece = jnp.sum(spread(piece, to_far, far), axis=0)
+        return spread(piece, to_col, peers).reshape(gram.shape)
 
     def body(weights, pattern, sketch):
         core = (lax.axis_index("row") % 2).astype(jnp.int32).reshape(1)

time: 153 us -> 149 us (0.974)
  blocking collectives: 114 us -> 111 us
    all_to_all x2, blocking collectives: 39.6 us -> 34.1 us  [the longest x1 24.2 us: to_far(): return lax.all_to_all(x, 'row', 0, 0, axis_index_groups=far_groups)]
    all_to_all x3, blocking collectives: 74.4 us -> 76.5 us  [to_col(): return lax.all_to_all(x, 'col', 0, 0)]
where the time goes in v3:
time: 149 us; the launch traced here: 148 us
  blocking collectives  111 us (74%)
  Pallas kernels  21.6 us (14%)
  starting transfers between devices  11.1 us (7%)
  local copies, waits for them, and re-layouts  3.02 us (2%)
  waiting for transfers between devices  1.84 us (1%)
    all_to_all x3, blocking collectives, to_col(): return lax.all_to_all(x, 'col', 0, 0)  76.5 us
    all_to_all x1, blocking collectives, to_far(): return lax.all_to_all(x, 'row', 0, 0, axis_index_groups=far_groups)  24.2 us
    pallas_call x1, Pallas kernels, basis(): pl.pallas_call(basis_kernel, out_shape=(in_vmem((rows.shape[0] // 2, rows...  18.5 us
    all_to_all x1, blocking collectives, to_near(): return lax.all_to_all(x, 'row', 0, 0, axis_index_groups=near_groups)  9.93 us
    ppermute x1, starting transfers between devices, body(): back = lax.ppermute(away, 'row', cores)  6.59 us
    ppermute x1, starting transfers between devices, body(): got = lax.ppermute(other, 'row', cores)  4.55 us
  transfers between devices with their start and end apart: 2, of which 2 were waited for; matrix products, arithmetic and copies ran while one was open for 0% of the time, Pallas kernels for 0%

profile of v3, /device:TPU:1, one launch (start us, length us, event | category | flops | bytes accessed | tf_op | source)
XLA Modules:
  0.0 148.4 jit_solution(18386046417914061220)
XLA Ops:
  0.0 0.0 copy-start
  0.0 1.3 copy-done
  1.3 0.0 copy-start.1
  1.3 1.0 copy-done.1
  2.3 0.0 copy-start.2
  2.3 0.7 copy-done.2
  3.0 1.6 %product.1 = f32[16,2,48,512]{3,2,1,0:T(8,128)S(1)} custom-call(s32[3,2,6]{2,1,0:T(2,128)S(1)} %bitcast.6, bf16[2,768,384]{2,1,0:T(8,128)(2,1)S(1)} %copy-done, bf16[384,512]{1,0:T(8,128)(2,1)S(1)} %copy-done.1), custom_call_target="tpu_custom_call" | custom-call | tf_op jit(solution)/shard_map/product/pallas_call | solution.py:140
  4.5 46.2 %all_to_all.25.parts_ref = f32[16,2,48,512]{3,2,1,0:T(8,128)S(1)} all-to-all(f32[16,2,48,512]{3,2,1,0:T(8,128)S(1)} %product.1), channel_id=1, replica_groups=mesh['row'=32,'col'=16] {'col'}, dimensions={0} | all-to-all | bytes 6291456 | tf_op jit(solution)/shard_map/all_to_all | solution.py:223
  50.7 0.1 total.1
  50.9 4.5 %collective-permute-start = (f32[48,512]{1,0:T(8,128)S(1)}, f32[48,512]{1,0:T(8,128)S(1)}, u32[]{:S(2)}, u32[]{:S(2)}) collective-permute-start(f32[48,512]{1,0:T(8,128)S(1)} %get-tuple-element.16), channel_id=1, source_target_pairs={{0,16},{16,0},{32,48},{48,32},{64,80},{80,64},{96,112},{112,96},{1... | collective-permute-start | bytes 294920 | tf_op jit(solution)/shard_map/ppermute | solution.py:244
  55.4 0.9 collective-permute-done.got_ref
  56.3 0.7 local_gram.1
  57.1 15.3 %all_to_all.26 = f32[16,80,128]{2,1,0:T(8,128)S(1)} all-to-all(f32[16,80,128]{2,1,0:T(8,128)S(1)} %bitcast.5), channel_id=1, replica_groups=mesh['row'=32,'col'=16] {'col'}, dimensions={0} | all-to-all | bytes 1310720 | tf_op jit(solution)/shard_map/all_to_all | solution.py:223
  72.4 9.9 %all_to_all.27 = f32[4,80,128]{2,1,0:T(8,128)S(1)} all-to-all(f32[4,80,128]{2,1,0:T(8,128)S(1)} %broadcast_in_dim.9), channel_id=1, replica_groups={{0,32,64,96},{16,48,80,112},{128,160,192,224},{144,176,208,240},{256,28..., dimensions={0} | all-to-all | bytes 327680 | tf_op jit(solution)/shard_map/all_to_all | solution.py:226
  82.4 24.2 %all_to_all.28 = f32[4,80,128]{2,1,0:T(8,128)S(1)} all-to-all(f32[4,80,128]{2,1,0:T(8,128)S(1)} %broadcast_in_dim.10), channel_id=1, replica_groups={{0,128,256,384},{16,144,272,400},{32,160,288,416},{48,176,304,432},{64,..., dimensions={0} | all-to-all | bytes 327680 | tf_op jit(solution)/shard_map/all_to_all | solution.py:229
  106.6 15.1 %all_to_all.29 = f32[16,80,128]{2,1,0:T(8,128)S(1)} all-to-all(f32[16,80,128]{2,1,0:T(8,128)S(1)} %broadcast_in_dim.11), channel_id=1, replica_groups=mesh['row'=32,'col'=16] {'col'}, dimensions={0} | all-to-all | bytes 1310720 | tf_op jit(solution)/shard_map/all_to_all | solution.py:223
  121.7 18.5 %basis.1 = (f32[48,512]{1,0:T(8,128)S(1)}, f32[48,512]{1,0:T(8,128)S(1)}) custom-call(f32[1280,128]{1,0:T(8,128)S(1)} %bitcast.4, f32[96,512]{1,0:T(8,128)S(1)} %get-tuple-element.18.rows_ref), custom_call_target="tpu_custom_call" | custom-call | tf_op jit(solution)/shard_map/basis/pallas_call | solution.py:98
  140.2 6.6 %collective-permute-start.1 = (f32[48,512]{1,0:T(8,128)S(1)}, f32[48,512]{1,0:T(8,128)S(1)}, u32[]{:S(2)}, u32[]{:S(2)}) collective-permute-start(f32[48,512]{1,0:T(8,128)S(1)} %get-tuple-element.20), channel_id=1, source_target_pairs={{0,16},{16,0},{32,48},{48,32},{64,80},{80,64},{96,112},{112,96},{1... | collective-permute-start | bytes 294920 | tf_op jit(solution)/shard_map/ppermute | solution.py:247
  146.8 0.9 collective-permute-done.1.back_ref
  147.7 0.7 merge.1
  (6 shorter events, 0.1 us)
Async XLA Ops:
  0.0 1.3 copy-start
  1.3 1.0 copy-start.1
  2.3 0.7 copy-start.2
  50.9 5.5 %collective-permute-start = (f32[48,512]{1,0:T(8,128)S(1)}, f32[48,512]{1,0:T(8,128)S(1)}, u32[]{:S(2)}, u32[]{:S(2)}) collective-permute-start(f32[48,512]{1,0:T(8,128)S(1)} %get-tuple-element.16), channel_id=1, source_target_pairs={{0,16},{16,0},{32,48},{48,32},{64,80},{80,64},{96,112},{112,96},{1... | collective-permute-start | bytes 294920 | tf_op jit(solution)/shard_map/ppermute | solution.py:244
  140.2 7.5 %collective-permute-start.1 = (f32[48,512]{1,0:T(8,128)S(1)}, f32[48,512]{1,0:T(8,128)S(1)}, u32[]{:S(2)}, u32[]{:S(2)}) collective-permute-start(f32[48,512]{1,0:T(8,128)S(1)} %get-tuple-element.20), channel_id=1, source_target_pairs={{0,16},{16,0},{32,48},{48,32},{64,80},{80,64},{96,112},{112,96},{1... | collective-permute-start | bytes 294920 | tf_op jit(solution)/shard_map/ppermute | solution.py:247

commit v4 on v3

--- a/solution.py
+++ b/solution.py
@@ -11,7 +11,7 @@
 BLOCK = 128
 LAYERS = 2
 SUP = 32
-PAN = 8
+PAN = 16
 GRANT = 24 << 20
 HI = lax.Precision.HIGHEST
 
@@ -22,8 +22,8 @@
     return lax.dot_general(a, b, (((0,), (0,)), ((), ())), precision=HI, preferred_element_type=jnp.float32)
 
 def inverse_factor(x_ref):
-    lane8 = lax.broadcasted_iota(jnp.int32, (PAN, BLOCK), 1)
-    row8 = lax.broadcasted_iota(jnp.int32, (PAN, BLOCK), 0)
+    lanes = lax.broadcasted_iota(jnp.int32, (PAN, BLOCK), 1)
+    rowis = lax.broadcasted_iota(jnp.int32, (PAN, BLOCK), 0)
     for first in range(0, BLOCK, SUP):
         rows = [x_ref[first + PAN * i : first + PAN * (i + 1), :] for i in range(SUP // PAN)]
         for p in range(SUP // PAN):
@@ -33,20 +33,21 @@
             for k in range(PAN):
                 pivot = jnp.broadcast_to(cols[0][k][k : k + 1, :], (PAN, BLOCK))
                 inv = 1.0 / pivot
-                diag = jnp.where(row8 == k, pivot, diag)
-                source = jnp.where(lane8 == lead + k, 1.0, jnp.broadcast_to(rows[p][k : k + 1, :], (PAN, BLOCK)))
-                heads = [jnp.broadcast_to(cols[0][m][k : k + 1, :], (PAN, BLOCK)) * inv for m in range(k + 1, PAN)]
+                diag = jnp.where(rowis == k, pivot, diag)
+                source = jnp.where(lanes == lead + k, 1.0, jnp.broadcast_to(rows[p][k : k + 1, :], (PAN, BLOCK)))
+                raw = [jnp.broadcast_to(cols[0][k][m : m + 1, :], (PAN, BLOCK)) for m in range(k + 1, PAN)]
                 for i in range(p, SUP // PAN):
                     col = cols[i - p][k]
                     if i == p:
-                        col = jnp.where(row8 > k, col, 0.0)
-                        keep = jnp.where((lane8 == lead + k) & (row8 > k), 0.0, rows[i])
-                        keep = jnp.where((lane8 == lead + k) & (row8 == k), 1.0, keep)
+                        col = jnp.where(rowis > k, col, 0.0)
+                        keep = jnp.where((lanes == lead + k) & (rowis > k), 0.0, rows[i])
+                        keep = jnp.where((lanes == lead + k) & (rowis == k), 1.0, keep)
                     else:
-                        keep = jnp.where(lane8 == lead + k, 0.0, rows[i])
-                    rows[i] = keep - (col * inv) * source
+                        keep = jnp.where(lanes == lead + k, 0.0, rows[i])
+                    scaled = col * inv
+                    rows[i] = keep - scaled * source
                     for m in range(k + 1, PAN):
-                        cols[i - p][m] = cols[i - p][m] - col * heads[m - k - 1]
+                        cols[i - p][m] = cols[i - p][m] - scaled * raw[m - k - 1]
             rows[p] = rows[p] * lax.rsqrt(diag)
         whole = jnp.concatenate(rows, axis=0)
         lane = lax.broadcasted_iota(jnp.int32, (SUP, BLOCK), 1)
@@ -55,11 +56,12 @@
         last = first + SUP
         if last < BLOCK:
             x_ref[first:last, :] = jnp.where(lane > row, 0.0, whole)
-            delta = tn(whole, low)
+            flip = whole.T
+            delta = jnp.concatenate([lax.dot_general(flip[r : r + SUP, :], low, (((1,), (0,)), ((), ())), precision=HI, preferred_element_type=jnp.float32) for r in range(last, BLOCK, SUP)], axis=0)
             lane_b = lax.broadcasted_iota(jnp.int32, (BLOCK - last, BLOCK), 1)
             below = x_ref[last:BLOCK, :]
             below = jnp.where((lane_b >= first) & (lane_b < last), 0.0, below)
-            x_ref[last:BLOCK, :] = below - delta[last:BLOCK, :]
+            x_ref[last:BLOCK, :] = below - delta
         else:
             x_ref[first:last, :] = low
     return x_ref[...]

time: 149 us -> 145 us (0.973)
  Pallas kernels: 21.6 us -> 18 us
    pallas_call x1, Pallas kernels: 18.5 us -> 14.8 us  [basis(): pl.pallas_call(basis_kernel, out_shape=(in_vmem((rows.shape[0] // 2, rows...]
where the time goes in v4:
time: 145 us
  blocking collectives  111 us (77%)
  Pallas kernels  18 us (12%)
  starting transfers between devices  11.1 us (8%)
  local copies, waits for them, and re-layouts  3.02 us (2%)
  waiting for transfers between devices  1.84 us (1%)
    all_to_all x3, blocking collectives, to_col(): return lax.all_to_all(x, 'col', 0, 0)  76.5 us
    all_to_all x1, blocking collectives, to_far(): return lax.all_to_all(x, 'row', 0, 0, axis_index_groups=far_groups)  24.2 us
    pallas_call x1, Pallas kernels, basis(): pl.pallas_call(basis_kernel, out_shape=(in_vmem((rows.shape[0] // 2, rows...  14.8 us
    all_to_all x1, blocking collectives, to_near(): return lax.all_to_all(x, 'row', 0, 0, axis_index_groups=near_groups)  9.93 us
    ppermute x1, starting transfers between devices, body(): back = lax.ppermute(away, 'row', cores)  6.59 us
    ppermute x1, starting transfers between devices, body(): got = lax.ppermute(other, 'row', cores)  4.55 us
    unnamed x6, local copies, waits for them, and re-layouts  2.95 us
  transfers between devices with their start and end apart: 2, of which 2 were waited for; matrix products, arithmetic and copies ran while one was open for 0% of the time, Pallas kernels for 0%

profile of v4, /device:TPU:1, one launch (start us, length us, event | category | flops | bytes accessed | tf_op | source)
XLA Modules:
  0.0 144.8 jit_solution(16850236425517588554)
XLA Ops:
  0.0 0.0 copy-start
  0.0 1.3 copy-done
  1.3 0.0 copy-start.1
  1.3 1.0 copy-done.1
  2.3 0.0 copy-start.2
  2.3 0.7 copy-done.2
  3.0 1.6 %product.1 = f32[16,2,48,512]{3,2,1,0:T(8,128)S(1)} custom-call(s32[3,2,6]{2,1,0:T(2,128)S(1)} %bitcast.6, bf16[2,768,384]{2,1,0:T(8,128)(2,1)S(1)} %copy-done, bf16[384,512]{1,0:T(8,128)(2,1)S(1)} %copy-done.1), custom_call_target="tpu_custom_call" | custom-call | tf_op jit(solution)/shard_map/product/pallas_call | solution.py:142
  4.5 46.2 %all_to_all.25.parts_ref = f32[16,2,48,512]{3,2,1,0:T(8,128)S(1)} all-to-all(f32[16,2,48,512]{3,2,1,0:T(8,128)S(1)} %product.1), channel_id=1, replica_groups=mesh['row'=32,'col'=16] {'col'}, dimensions={0} | all-to-all | bytes 6291456 | tf_op jit(solution)/shard_map/all_to_all | solution.py:225
  50.7 0.1 total.1
  50.9 4.5 %collective-permute-start = (f32[48,512]{1,0:T(8,128)S(1)}, f32[48,512]{1,0:T(8,128)S(1)}, u32[]{:S(2)}, u32[]{:S(2)}) collective-permute-start(f32[48,512]{1,0:T(8,128)S(1)} %get-tuple-element.16), channel_id=1, source_target_pairs={{0,16},{16,0},{32,48},{48,32},{64,80},{80,64},{96,112},{112,96},{1... | collective-permute-start | bytes 294920 | tf_op jit(solution)/shard_map/ppermute | solution.py:246
  55.4 0.9 collective-permute-done.got_ref
  56.3 0.7 local_gram.1
  57.1 15.3 %all_to_all.26 = f32[16,80,128]{2,1,0:T(8,128)S(1)} all-to-all(f32[16,80,128]{2,1,0:T(8,128)S(1)} %bitcast.5), channel_id=1, replica_groups=mesh['row'=32,'col'=16] {'col'}, dimensions={0} | all-to-all | bytes 1310720 | tf_op jit(solution)/shard_map/all_to_all | solution.py:225
  72.4 9.9 %all_to_all.27 = f32[4,80,128]{2,1,0:T(8,128)S(1)} all-to-all(f32[4,80,128]{2,1,0:T(8,128)S(1)} %broadcast_in_dim.9), channel_id=1, replica_groups={{0,32,64,96},{16,48,80,112},{128,160,192,224},{144,176,208,240},{256,28..., dimensions={0} | all-to-all | bytes 327680 | tf_op jit(solution)/shard_map/all_to_all | solution.py:228
  82.4 24.2 %all_to_all.28 = f32[4,80,128]{2,1,0:T(8,128)S(1)} all-to-all(f32[4,80,128]{2,1,0:T(8,128)S(1)} %broadcast_in_dim.10), channel_id=1, replica_groups={{0,128,256,384},{16,144,272,400},{32,160,288,416},{48,176,304,432},{64,..., dimensions={0} | all-to-all | bytes 327680 | tf_op jit(solution)/shard_map/all_to_all | solution.py:231
  106.6 15.1 %all_to_all.29 = f32[16,80,128]{2,1,0:T(8,128)S(1)} all-to-all(f32[16,80,128]{2,1,0:T(8,128)S(1)} %broadcast_in_dim.11), channel_id=1, replica_groups=mesh['row'=32,'col'=16] {'col'}, dimensions={0} | all-to-all | bytes 1310720 | tf_op jit(solution)/shard_map/all_to_all | solution.py:225
  121.7 14.8 %basis.1 = (f32[48,512]{1,0:T(8,128)S(1)}, f32[48,512]{1,0:T(8,128)S(1)}) custom-call(f32[1280,128]{1,0:T(8,128)S(1)} %bitcast.4, f32[96,512]{1,0:T(8,128)S(1)} %get-tuple-element.18.rows_ref), custom_call_target="tpu_custom_call" | custom-call | tf_op jit(solution)/shard_map/basis/pallas_call | solution.py:100
  136.5 6.6 %collective-permute-start.1 = (f32[48,512]{1,0:T(8,128)S(1)}, f32[48,512]{1,0:T(8,128)S(1)}, u32[]{:S(2)}, u32[]{:S(2)}) collective-permute-start(f32[48,512]{1,0:T(8,128)S(1)} %get-tuple-element.20), channel_id=1, source_target_pairs={{0,16},{16,0},{32,48},{48,32},{64,80},{80,64},{96,112},{112,96},{1... | collective-permute-start | bytes 294920 | tf_op jit(solution)/shard_map/ppermute | solution.py:249
  143.1 0.9 collective-permute-done.1.back_ref
  144.1 0.7 merge.1
  (6 shorter events, 0.1 us)
Async XLA Ops:
  0.0 1.3 copy-start
  1.3 1.0 copy-start.1
  2.3 0.7 copy-start.2
  50.9 5.5 %collective-permute-start = (f32[48,512]{1,0:T(8,128)S(1)}, f32[48,512]{1,0:T(8,128)S(1)}, u32[]{:S(2)}, u32[]{:S(2)}) collective-permute-start(f32[48,512]{1,0:T(8,128)S(1)} %get-tuple-element.16), channel_id=1, source_target_pairs={{0,16},{16,0},{32,48},{48,32},{64,80},{80,64},{96,112},{112,96},{1... | collective-permute-start | bytes 294920 | tf_op jit(solution)/shard_map/ppermute | solution.py:246
  136.5 7.5 %collective-permute-start.1 = (f32[48,512]{1,0:T(8,128)S(1)}, f32[48,512]{1,0:T(8,128)S(1)}, u32[]{:S(2)}, u32[]{:S(2)}) collective-permute-start(f32[48,512]{1,0:T(8,128)S(1)} %get-tuple-element.20), channel_id=1, source_target_pairs={{0,16},{16,0},{32,48},{48,32},{64,80},{80,64},{96,112},{112,96},{1... | collective-permute-start | bytes 294920 | tf_op jit(solution)/shard_map/ppermute | solution.py:249

commit v5 on v4

--- a/solution.py
+++ b/solution.py
@@ -13,6 +13,7 @@
 SUP = 32
 PAN = 16
 GRANT = 24 << 20
+PARTS = 2
 HI = lax.Precision.HIGHEST
 
 
@@ -120,33 +121,55 @@
     return pltpu.with_memory_space_constraint(x, pltpu.VMEM)
 
 
-def product_kernel(pattern_ref, weights_ref, sketch_ref, out_ref):
+def product_kernel(pattern_hbm, weights_hbm, sketch_hbm, out_ref, pattern_ref, weights_ref, sketch_ref, sems):
     layers, height, width = weights_ref.shape
     peers, _, share, rank = out_ref.shape
+    part = height // PARTS
+    copies = [
+        pltpu.make_async_copy(pattern_hbm, pattern_ref, sems.at[0]),
+        pltpu.make_async_copy(sketch_hbm, sketch_ref, sems.at[1]),
+    ]
     for layer in range(layers):
-        strips = []
-        for i in range(height // BLOCK):
-            parts = []
-            for j in range(width // BLOCK):
-                block = weights_ref[layer, i * BLOCK : (i + 1) * BLOCK, j * BLOCK : (j + 1) * BLOCK]
-                parts.append(jnp.where(pattern_ref[j, layer, i] == 1, jnp.zeros_like(block), block))
-            strips.append(jnp.concatenate(parts, axis=1))
-        leftover = jnp.concatenate(strips, axis=0)
-        product = jnp.dot(leftover, sketch_ref[...], preferred_element_type=jnp.float32)
-        out_ref[:, layer] = product.reshape(peers, share, rank)
+        for h in range(PARTS):
+            rows = pl.ds(h * part, part)
+            copies.append(pltpu.make_async_copy(weights_hbm.at[layer, rows], weights_ref.at[layer, rows], sems.at[len(copies)]))
+    for copy in copies:
+        copy.start()
+    copies[0].wait()
+    copies[1].wait()
+    for layer in range(layers):
+        for h in range(PARTS):
+            copies[2 + layer * PARTS + h].wait()
+            strips = []
+            for i in range(h * part // BLOCK, (h + 1) * part // BLOCK):
+                parts = []
+                for j in range(width // BLOCK):
+                    block = weights_ref[layer, i * BLOCK : (i + 1) * BLOCK, j * BLOCK : (j + 1) * BLOCK]
+                    parts.append(jnp.where(pattern_ref[j, layer, i] == 1, jnp.zeros_like(block), block))
+                strips.append(jnp.concatenate(parts, axis=1))
+            leftover = jnp.concatenate(strips, axis=0)
+            product = jnp.dot(leftover, sketch_ref[...], preferred_element_type=jnp.float32)
+            out_ref[h * peers // PARTS : (h + 1) * peers // PARTS, layer] = product.reshape(peers // PARTS, share, rank)
 
 
 def product(weights, pattern, sketch, peers):
     layers, height, width = weights.shape
     rank = sketch.shape[1]
+    anywhere = pl.BlockSpec(memory_space=pltpu.HBM)
     return pl.pallas_call(
         product_kernel,
         out_shape=in_vmem((peers, layers, height // peers, rank)),
-        in_specs=[pl.BlockSpec(memory_space=pltpu.SMEM), vmem(), vmem()],
+        in_specs=[anywhere] * 3,
         out_specs=vmem(),
+        scratch_shapes=[
+            pltpu.SMEM(pattern.shape, jnp.int32),
+            pltpu.VMEM(weights.shape, weights.dtype),
+            pltpu.VMEM(sketch.shape, sketch.dtype),
+            pltpu.SemaphoreType.DMA((2 + layers * PARTS,)),
+        ],
         compiler_params=pltpu.CompilerParams(vmem_limit_bytes=GRANT),
         name="product",
-    )(pattern, weights, sketch)
+    )(*(pltpu.with_memory_space_constraint(x, pltpu.HBM) for x in (pattern, weights, sketch)))
 
 
 def total_kernel(core_ref, parts_ref, mine_ref, other_ref):

time: 145 us -> 143 us (0.986)
  local copies, waits for them, and re-layouts: 3.02 us -> 0.07 us
    unnamed x6 -> x0, local copies, waits for them, and re-layouts: 2.95 us -> none
where the time goes in v5:
time: 143 us
  blocking collectives  111 us (78%)
  Pallas kernels  19 us (13%)
  starting transfers between devices  11.1 us (8%)
  waiting for transfers between devices  1.84 us (1%)
    all_to_all x3, blocking collectives, to_col(): return lax.all_to_all(x, 'col', 0, 0)  76.7 us
    all_to_all x1, blocking collectives, to_far(): return lax.all_to_all(x, 'row', 0, 0, axis_index_groups=far_groups)  24.2 us
    pallas_call x1, Pallas kernels, basis(): pl.pallas_call(basis_kernel, out_shape=(in_vmem((rows.shape[0] // 2, rows...  14.8 us
    all_to_all x1, blocking collectives, to_near(): return lax.all_to_all(x, 'row', 0, 0, axis_index_groups=near_groups)  9.86 us
    ppermute x1, starting transfers between devices, body(): back = lax.ppermute(away, 'row', cores)  6.59 us
    ppermute x1, starting transfers between devices, body(): got = lax.ppermute(other, 'row', cores)  4.53 us
  transfers between devices with their start and end apart: 2, of which 2 were waited for; matrix products, arithmetic and copies ran while one was open for 0% of the time, Pallas kernels for 0%

profile of v5, /device:TPU:1, one launch (start us, length us, event | category | flops | bytes accessed | tf_op | source)
XLA Modules:
  0.0 142.9 jit_solution(13220974805103324865)
XLA Ops:
  0.0 2.6 %product.1 = f32[16,2,48,512]{3,2,1,0:T(8,128)S(1)} custom-call(s32[3,2,6]{2,1,0:T(2,128)} %bitcast.6, bf16[2,768,384]{2,1,0:T(8,128)(2,1)} %weights_hbm.1, bf16[384,512]{1,0:T(8,128)(2,1)} %sketch_hbm.1), custom_call_target="tpu_custom_call" | custom-call | tf_op jit(solution)/shard_map/product/pallas_call | solution.py:159
  2.6 46.3 %all_to_all.25.parts_ref = f32[16,2,48,512]{3,2,1,0:T(8,128)S(1)} all-to-all(f32[16,2,48,512]{3,2,1,0:T(8,128)S(1)} %product.1), channel_id=1, replica_groups=mesh['row'=32,'col'=16] {'col'}, dimensions={0} | all-to-all | bytes 6291456 | tf_op jit(solution)/shard_map/all_to_all | solution.py:248
  48.9 0.1 total.1
  49.1 4.5 %collective-permute-start = (f32[48,512]{1,0:T(8,128)S(1)}, f32[48,512]{1,0:T(8,128)S(1)}, u32[]{:S(2)}, u32[]{:S(2)}) collective-permute-start(f32[48,512]{1,0:T(8,128)S(1)} %get-tuple-element.16), channel_id=1, source_target_pairs={{0,16},{16,0},{32,48},{48,32},{64,80},{80,64},{96,112},{112,96},{1... | collective-permute-start | bytes 294920 | tf_op jit(solution)/shard_map/ppermute | solution.py:269
  53.6 0.9 collective-permute-done.got_ref
  54.5 0.7 local_gram.1
  55.3 15.3 %all_to_all.26 = f32[16,80,128]{2,1,0:T(8,128)S(1)} all-to-all(f32[16,80,128]{2,1,0:T(8,128)S(1)} %bitcast.5), channel_id=1, replica_groups=mesh['row'=32,'col'=16] {'col'}, dimensions={0} | all-to-all | bytes 1310720 | tf_op jit(solution)/shard_map/all_to_all | solution.py:248
  70.6 9.9 %all_to_all.27 = f32[4,80,128]{2,1,0:T(8,128)S(1)} all-to-all(f32[4,80,128]{2,1,0:T(8,128)S(1)} %broadcast_in_dim.9), channel_id=1, replica_groups={{0,32,64,96},{16,48,80,112},{128,160,192,224},{144,176,208,240},{256,28..., dimensions={0} | all-to-all | bytes 327680 | tf_op jit(solution)/shard_map/all_to_all | solution.py:251
  80.5 24.2 %all_to_all.28 = f32[4,80,128]{2,1,0:T(8,128)S(1)} all-to-all(f32[4,80,128]{2,1,0:T(8,128)S(1)} %broadcast_in_dim.10), channel_id=1, replica_groups={{0,128,256,384},{16,144,272,400},{32,160,288,416},{48,176,304,432},{64,..., dimensions={0} | all-to-all | bytes 327680 | tf_op jit(solution)/shard_map/all_to_all | solution.py:254
  104.7 15.1 %all_to_all.29 = f32[16,80,128]{2,1,0:T(8,128)S(1)} all-to-all(f32[16,80,128]{2,1,0:T(8,128)S(1)} %broadcast_in_dim.11), channel_id=1, replica_groups=mesh['row'=32,'col'=16] {'col'}, dimensions={0} | all-to-all | bytes 1310720 | tf_op jit(solution)/shard_map/all_to_all | solution.py:248
  119.8 14.8 %basis.1 = (f32[48,512]{1,0:T(8,128)S(1)}, f32[48,512]{1,0:T(8,128)S(1)}) custom-call(f32[1280,128]{1,0:T(8,128)S(1)} %bitcast.4, f32[96,512]{1,0:T(8,128)S(1)} %get-tuple-element.18.rows_ref), custom_call_target="tpu_custom_call" | custom-call | tf_op jit(solution)/shard_map/basis/pallas_call | solution.py:101
  134.6 6.6 %collective-permute-start.1 = (f32[48,512]{1,0:T(8,128)S(1)}, f32[48,512]{1,0:T(8,128)S(1)}, u32[]{:S(2)}, u32[]{:S(2)}) collective-permute-start(f32[48,512]{1,0:T(8,128)S(1)} %get-tuple-element.20), channel_id=1, source_target_pairs={{0,16},{16,0},{32,48},{48,32},{64,80},{80,64},{96,112},{112,96},{1... | collective-permute-start | bytes 294920 | tf_op jit(solution)/shard_map/ppermute | solution.py:272
  141.2 0.9 collective-permute-done.1.back_ref
  142.2 0.7 merge.1
  (6 shorter events, 0.1 us)
Async XLA Ops:
  49.1 5.5 %collective-permute-start = (f32[48,512]{1,0:T(8,128)S(1)}, f32[48,512]{1,0:T(8,128)S(1)}, u32[]{:S(2)}, u32[]{:S(2)}) collective-permute-start(f32[48,512]{1,0:T(8,128)S(1)} %get-tuple-element.16), channel_id=1, source_target_pairs={{0,16},{16,0},{32,48},{48,32},{64,80},{80,64},{96,112},{112,96},{1... | collective-permute-start | bytes 294920 | tf_op jit(solution)/shard_map/ppermute | solution.py:269
  134.6 7.5 %collective-permute-start.1 = (f32[48,512]{1,0:T(8,128)S(1)}, f32[48,512]{1,0:T(8,128)S(1)}, u32[]{:S(2)}, u32[]{:S(2)}) collective-permute-start(f32[48,512]{1,0:T(8,128)S(1)} %get-tuple-element.20), channel_id=1, source_target_pairs={{0,16},{16,0},{32,48},{48,32},{64,80},{80,64},{96,112},{112,96},{1... | collective-permute-start | bytes 294920 | tf_op jit(solution)/shard_map/ppermute | solution.py:272

commit v6 on v5

--- a/solution.py
+++ b/solution.py
@@ -70,10 +70,11 @@
 def start_of(n, j):
     return BLOCK * sum(n - i for i in range(j))
 
-def basis_kernel(gram_ref, rows_ref, own_ref, away_ref, a_ref, s_ref, x_ref):
-    n = rows_ref.shape[1] // BLOCK
+def basis_kernel(gram_ref, rows_ref, out_ref, a_ref, s_ref, x_ref):
+    count, share, rank = rows_ref.shape
+    n = rank // BLOCK
     a_ref[...] = gram_ref[...]
-    s_ref[...] = rows_ref[...]
+    s_ref[...] = rows_ref[...].reshape(count * share, rank)
     for k in range(n):
         base = start_of(n, k)
         x_ref[...] = a_ref[base : base + BLOCK, :]
@@ -86,9 +87,7 @@
             stacked = tail
         panel = nt(stacked, w)
         solved = panel[below:, :] * float(M)
-        share = solved.shape[0] // 2
-        own_ref[:, k * BLOCK : (k + 1) * BLOCK] = solved[:share, :]
-        away_ref[:, k * BLOCK : (k + 1) * BLOCK] = solved[share:, :]
+        out_ref[:, :, k * BLOCK : (k + 1) * BLOCK] = solved.reshape(count, share, BLOCK)
         for j in range(k + 1, n):
             off = (j - k - 1) * BLOCK
             update = nt(panel[off:, :], panel[off : off + BLOCK, :])
@@ -98,13 +97,14 @@
             s_ref[:, j * BLOCK : (j + 1) * BLOCK] = s_ref[:, j * BLOCK : (j + 1) * BLOCK] - update[height:, :]
 
 def basis(gram, rows):
+    count, share, rank = rows.shape
     return pl.pallas_call(
         basis_kernel,
-        out_shape=(in_vmem((rows.shape[0] // 2, rows.shape[1])),) * 2,
+        out_shape=in_vmem(rows.shape),
         in_specs=[vmem(), vmem()],
-        out_specs=(vmem(), vmem()),
-        compiler_params=pltpu.CompilerParams(vmem_limit_bytes=GRANT),
-        scratch_shapes=[pltpu.VMEM(gram.shape, jnp.float32), pltpu.VMEM(rows.shape, jnp.float32), pltpu.VMEM((BLOCK, BLOCK), jnp.float32)],
+        out_specs=vmem(),
+        scratch_shapes=[pltpu.VMEM(gram.shape, jnp.float32), pltpu.VMEM((count * share, rank), jnp.float32), pltpu.VMEM((BLOCK, BLOCK), jnp.float32)],
+        compiler_params=pltpu.CompilerParams(vmem_limit_bytes=GRANT),
         name="basis",
     )(gram, rows)
 
@@ -172,73 +172,47 @@
     )(*(pltpu.with_memory_space_constraint(x, pltpu.HBM) for x in (pattern, weights, sketch)))
 
 
-def total_kernel(core_ref, parts_ref, mine_ref, other_ref):
-    core = core_ref[0]
-    peers = parts_ref.shape[0]
-    for layer, out_ref in ((core, mine_ref), (1 - core, other_ref)):
-        total = parts_ref[0, layer]
-        for peer in range(1, peers):
-            total = total + parts_ref[peer, layer]
-        out_ref[...] = total
-
-
-def total(core, parts):
-    shape = in_vmem(parts.shape[2:])
+def total_kernel(parts_ref, out_ref):
+    total = parts_ref[0]
+    for peer in range(1, parts_ref.shape[0]):
+        total = total + parts_ref[peer]
+    out_ref[...] = total
+
+
+def total(parts):
     return pl.pallas_call(
         total_kernel,
-        out_shape=(shape, shape),
-        in_specs=[pl.BlockSpec(memory_space=pltpu.SMEM), vmem()],
-        out_specs=(vmem(), vmem()),
+        out_shape=in_vmem(parts.shape[1:]),
+        in_specs=[vmem()],
+        out_specs=vmem(),
         compiler_params=pltpu.CompilerParams(vmem_limit_bytes=GRANT),
         name="total",
-    )(core, held(parts))
-
-
-def merge_kernel(core_ref, own_ref, back_ref, out_ref):
-    core = core_ref[0]
-    out_ref[core] = own_ref[...]
-    out_ref[1 - core] = back_ref[...]
-
-
-def merge(core, own, back):
-    return pl.pallas_call(
-        merge_kernel,
-        out_shape=jax.ShapeDtypeStruct((LAYERS, *own.shape), jnp.float32),
-        in_specs=[pl.BlockSpec(memory_space=pltpu.SMEM), vmem(), vmem()],
-        out_specs=vmem(),
-        compiler_params=pltpu.CompilerParams(vmem_limit_bytes=GRANT),
-        name="merge",
-    )(core, held(own), held(back))
-
-
-def gram_kernel(mine_ref, got_ref, gram_ref, rows_ref):
-    rows = jnp.concatenate([mine_ref[...], got_ref[...]], axis=0)
-    rows_ref[...] = rows
+    )(held(parts))
+
+
+def gram_kernel(rows_ref, gram_ref):
+    rows = rows_ref[...].reshape(-1, rows_ref.shape[-1])
     n = rows.shape[1] // BLOCK
     for j in range(n):
         to = start_of(n, j)
         gram_ref[to : to + (n - j) * BLOCK, :] = tn(rows[:, j * BLOCK :], rows[:, j * BLOCK : (j + 1) * BLOCK])
 
 
-def local_gram(mine, got):
-    share, rank = mine.shape
-    n = rank // BLOCK
+def local_gram(rows):
+    n = rows.shape[-1] // BLOCK
     return pl.pallas_call(
         gram_kernel,
-        out_shape=(
-            in_vmem((start_of(n, n), BLOCK)),
-            in_vmem((2 * share, rank)),
-        ),
-        in_specs=[vmem(), vmem()],
-        out_specs=(vmem(), vmem()),
+        out_shape=in_vmem((start_of(n, n), BLOCK)),
+        in_specs=[vmem()],
+        out_specs=vmem(),
         compiler_params=pltpu.CompilerParams(vmem_limit_bytes=GRANT),
         name="local_gram",
-    )(held(mine), held(got))
+    )(rows)
 
 
 def make_body(row_size, peers):
     chips = row_size // 2
-    cores = [(2 * z + c, 2 * z + 1 - c) for z in range(chips) for c in range(2)]
+    pairs = [[2 * z, 2 * z + 1] for z in range(chips)]
     near = math.isqrt(chips)
     far = chips // near
     near_groups = [[2 * (h * near + l) + c for l in range(near)] for h in range(far) for c in range(2)]
@@ -246,6 +220,9 @@
 
     def to_col(x):
         return lax.all_to_all(x, "col", 0, 0)
+
+    def swap(x):
+        return lax.all_to_all(x, "row", 0, 0, axis_index_groups=pairs)
 
     def to_near(x):
         return lax.all_to_all(x, "row", 0, 0, axis_index_groups=near_groups)
@@ -263,14 +240,9 @@
         return spread(piece, to_col, peers).reshape(gram.shape)
 
     def body(weights, pattern, sketch):
-        core = (lax.axis_index("row") % 2).astype(jnp.int32).reshape(1)
-        pattern, core = lax.optimization_barrier((pattern.transpose(2, 0, 1), core))
-        mine, other = total(core, to_col(product(weights, pattern, sketch, peers)))
-        got = lax.ppermute(other, "row", cores)
-        gram, rows = local_gram(mine, got)
-        own, away = basis(held(summed_gram(gram)), held(rows))
-        back = lax.ppermute(away, "row", cores)
-        return merge(core, own, back)
+        sampled = total(to_col(product(weights, pattern.transpose(2, 0, 1), sketch, peers)))
+        rows = held(swap(sampled))
+        return swap(basis(held(summed_gram(local_gram(rows))), rows))
 
     return body
 

time: 143 us -> 145 us (1.014)
  blocking collectives: 111 us -> 125 us
  starting transfers between devices: 11.1 us -> 0 us
  waiting for transfers between devices: 1.84 us -> 0 us
    all_to_all x0 -> x2, blocking collectives: none -> 14.4 us  [swap(): return lax.all_to_all(x, 'row', 0, 0, axis_index_groups=pairs)]
    ppermute x2 -> x0, starting transfers between devices: 11.1 us -> none  [the longest x1 6.59 us: body(): back = lax.ppermute(away, 'row', cores)]
    ppermute x2 -> x0, waiting for transfers between devices: 1.84 us -> none  [the longest x1 0.92 us: body(): got = lax.ppermute(other, 'row', cores)]
    pallas_call x4 -> x3, Pallas kernels: 16.4 us -> 15.7 us  [the longest x1 14.8 us: basis(): pl.pallas_call(basis_kernel, out_shape=in_vmem(rows.shape), in_specs=[vme...]
  transfers between devices with their start and end apart: 2 -> 0, of which waited for: 2 -> 0; matrix products, arithmetic and copies ran while one was open for 0% -> 0% of each run, Pallas kernels for 0% -> 0%
where the time goes in v6:
time: 145 us; the launch traced here: 144 us
  blocking collectives  125 us (86%)
  Pallas kernels  18.3 us (13%)
    all_to_all x3, blocking collectives, to_col(): return lax.all_to_all(x, 'col', 0, 0)  76.7 us
    all_to_all x1, blocking collectives, to_far(): return lax.all_to_all(x, 'row', 0, 0, axis_index_groups=far_groups)  24.2 us
    pallas_call x1, Pallas kernels, basis(): pl.pallas_call(basis_kernel, out_shape=in_vmem(rows.shape), in_specs=[vme...  14.8 us
    all_to_all x2, blocking collectives, swap(): return lax.all_to_all(x, 'row', 0, 0, axis_index_groups=pairs)  14.4 us
    all_to_all x1, blocking collectives, to_near(): return lax.all_to_all(x, 'row', 0, 0, axis_index_groups=near_groups)  9.86 us

profile of v6, /device:TPU:1, one launch (start us, length us, event | category | flops | bytes accessed | tf_op | source)
XLA Modules:
  0.0 144.2 jit_solution(14182150325144468497)
XLA Ops:
  0.0 2.6 %product.1 = f32[16,2,48,512]{3,2,1,0:T(8,128)S(1)} custom-call(s32[3,2,6]{2,1,0:T(2,128)} %bitcast.5, bf16[2,768,384]{2,1,0:T(8,128)(2,1)} %weights_hbm.1, bf16[384,512]{1,0:T(8,128)(2,1)} %sketch_hbm.1), custom_call_target="tpu_custom_call" | custom-call | tf_op jit(solution)/shard_map/product/pallas_call | solution.py:159
  2.6 46.3 %all_to_all.35.parts_ref = f32[16,2,48,512]{3,2,1,0:T(8,128)S(1)} all-to-all(f32[16,2,48,512]{3,2,1,0:T(8,128)S(1)} %product.1), channel_id=1, replica_groups=mesh['row'=32,'col'=16] {'col'}, dimensions={0} | all-to-all | bytes 6291456 | tf_op jit(solution)/shard_map/all_to_all | solution.py:222
  48.9 0.1 total.1
  49.1 6.2 %all_to_all.36.rows_ref = f32[2,48,512]{2,1,0:T(8,128)S(1)} all-to-all(f32[2,48,512]{2,1,0:T(8,128)S(1)} %total.1), channel_id=1, replica_groups={{0,16},{32,48},{64,80},{96,112},{128,144},{160,176},{192,208},{224,240}..., dimensions={0} | all-to-all | bytes 393216 | tf_op jit(solution)/shard_map/all_to_all | solution.py:225
  55.2 0.7 local_gram.1
  56.0 15.3 %all_to_all.37 = f32[16,80,128]{2,1,0:T(8,128)S(1)} all-to-all(f32[16,80,128]{2,1,0:T(8,128)S(1)} %bitcast.4), channel_id=1, replica_groups=mesh['row'=32,'col'=16] {'col'}, dimensions={0} | all-to-all | bytes 1310720 | tf_op jit(solution)/shard_map/all_to_all | solution.py:222
  71.3 9.9 %all_to_all.38 = f32[4,80,128]{2,1,0:T(8,128)S(1)} all-to-all(f32[4,80,128]{2,1,0:T(8,128)S(1)} %broadcast_in_dim.9), channel_id=1, replica_groups={{0,32,64,96},{16,48,80,112},{128,160,192,224},{144,176,208,240},{256,28..., dimensions={0} | all-to-all | bytes 327680 | tf_op jit(solution)/shard_map/all_to_all | solution.py:228
  81.2 24.2 %all_to_all.39 = f32[4,80,128]{2,1,0:T(8,128)S(1)} all-to-all(f32[4,80,128]{2,1,0:T(8,128)S(1)} %broadcast_in_dim.10), channel_id=1, replica_groups={{0,128,256,384},{16,144,272,400},{32,160,288,416},{48,176,304,432},{64,..., dimensions={0} | all-to-all | bytes 327680 | tf_op jit(solution)/shard_map/all_to_all | solution.py:231
  105.4 15.1 %all_to_all.40 = f32[16,80,128]{2,1,0:T(8,128)S(1)} all-to-all(f32[16,80,128]{2,1,0:T(8,128)S(1)} %broadcast_in_dim.11), channel_id=1, replica_groups=mesh['row'=32,'col'=16] {'col'}, dimensions={0} | all-to-all | bytes 1310720 | tf_op jit(solution)/shard_map/all_to_all | solution.py:222
  120.5 14.8 %basis.1 = f32[2,48,512]{2,1,0:T(8,128)S(1)} custom-call(f32[1280,128]{1,0:T(8,128)S(1)} %bitcast.3, f32[2,48,512]{2,1,0:T(8,128)S(1)} %all_to_all.36.rows_ref), custom_call_target="tpu_custom_call" | custom-call | tf_op jit(solution)/shard_map/basis/pallas_call | solution.py:101
  135.3 8.2 %all_to_all.41 = f32[2,48,512]{2,1,0:T(8,128)S(1)} all-to-all(f32[2,48,512]{2,1,0:T(8,128)S(1)} %basis.1), channel_id=1, replica_groups={{0,16},{32,48},{64,80},{96,112},{128,144},{160,176},{192,208},{224,240}..., dimensions={0} | all-to-all | bytes 393216 | tf_op jit(solution)/shard_map/all_to_all | solution.py:225
  143.6 0.7 copy.5
  (6 shorter events, 0.1 us)

commit v7 on v5

--- a/solution.py
+++ b/solution.py
@@ -258,8 +258,8 @@
 
     def summed_gram(gram):
         piece = jnp.sum(to_col(gram.reshape(peers, gram.shape[0] // peers, BLOCK)), axis=0)
+        piece = jnp.sum(spread(piece, to_far, far), axis=0)
         piece = jnp.sum(spread(piece, to_near, near), axis=0)
-        piece = jnp.sum(spread(piece, to_far, far), axis=0)
         return spread(piece, to_col, peers).reshape(gram.shape)
 
     def body(weights, pattern, sketch):

time: 143 us -> 145 us (1.014)
  starting transfers between devices: 11.1 us -> 12.7 us
    all_to_all x1, blocking collectives: 24.2 us -> 27.2 us  [to_far(): return lax.all_to_all(x, 'row', 0, 0, axis_index_groups=far_groups)]
    all_to_all x1, blocking collectives: 9.86 us -> 8.26 us  [to_near(): return lax.all_to_all(x, 'row', 0, 0, axis_index_groups=near_groups)]
    ppermute x1, starting transfers between devices: 6.59 us -> 8.13 us  [body(): back = lax.ppermute(away, 'row', cores)]
where the time goes in v7:
time: 145 us
  blocking collectives  111 us (77%)
  Pallas kernels  19 us (13%)
  starting transfers between devices  12.7 us (9%)
  waiting for transfers between devices  1.84 us (1%)
    all_to_all x3, blocking collectives, to_col(): return lax.all_to_all(x, 'col', 0, 0)  75.3 us
    all_to_all x1, blocking collectives, to_far(): return lax.all_to_all(x, 'row', 0, 0, axis_index_groups=far_groups)  27.2 us
    pallas_call x1, Pallas kernels, basis(): pl.pallas_call(basis_kernel, out_shape=(in_vmem((rows.shape[0] // 2, rows...  14.8 us
    all_to_all x1, blocking collectives, to_near(): return lax.all_to_all(x, 'row', 0, 0, axis_index_groups=near_groups)  8.26 us
    ppermute x1, starting transfers between devices, body(): back = lax.ppermute(away, 'row', cores)  8.13 us
    ppermute x1, starting transfers between devices, body(): got = lax.ppermute(other, 'row', cores)  4.53 us
  transfers between devices with their start and end apart: 2, of which 2 were waited for; matrix products, arithmetic and copies ran while one was open for 0% of the time, Pallas kernels for 0%

profile of v7, /device:TPU:1, one launch (start us, length us, event | category | flops | bytes accessed | tf_op | source)
XLA Modules:
  0.0 144.6 jit_solution(10504268721063140497)
XLA Ops:
  0.0 2.6 %product.1 = f32[16,2,48,512]{3,2,1,0:T(8,128)S(1)} custom-call(s32[3,2,6]{2,1,0:T(2,128)} %bitcast.6, bf16[2,768,384]{2,1,0:T(8,128)(2,1)} %weights_hbm.1, bf16[384,512]{1,0:T(8,128)(2,1)} %sketch_hbm.1), custom_call_target="tpu_custom_call" | custom-call | tf_op jit(solution)/shard_map/product/pallas_call | solution.py:159
  2.6 46.3 %all_to_all.25.parts_ref = f32[16,2,48,512]{3,2,1,0:T(8,128)S(1)} all-to-all(f32[16,2,48,512]{3,2,1,0:T(8,128)S(1)} %product.1), channel_id=1, replica_groups=mesh['row'=32,'col'=16] {'col'}, dimensions={0} | all-to-all | bytes 6291456 | tf_op jit(solution)/shard_map/all_to_all | solution.py:248
  48.9 0.1 total.1
  49.1 4.5 %collective-permute-start = (f32[48,512]{1,0:T(8,128)S(1)}, f32[48,512]{1,0:T(8,128)S(1)}, u32[]{:S(2)}, u32[]{:S(2)}) collective-permute-start(f32[48,512]{1,0:T(8,128)S(1)} %get-tuple-element.16), channel_id=1, source_target_pairs={{0,16},{16,0},{32,48},{48,32},{64,80},{80,64},{96,112},{112,96},{1... | collective-permute-start | bytes 294920 | tf_op jit(solution)/shard_map/ppermute | solution.py:269
  53.6 0.9 collective-permute-done.got_ref
  54.5 0.7 local_gram.1
  55.3 15.3 %all_to_all.26 = f32[16,80,128]{2,1,0:T(8,128)S(1)} all-to-all(f32[16,80,128]{2,1,0:T(8,128)S(1)} %bitcast.5), channel_id=1, replica_groups=mesh['row'=32,'col'=16] {'col'}, dimensions={0} | all-to-all | bytes 1310720 | tf_op jit(solution)/shard_map/all_to_all | solution.py:248
  70.6 27.2 %all_to_all.27 = f32[4,80,128]{2,1,0:T(8,128)S(1)} all-to-all(f32[4,80,128]{2,1,0:T(8,128)S(1)} %broadcast_in_dim.9), channel_id=1, replica_groups={{0,128,256,384},{16,144,272,400},{32,160,288,416},{48,176,304,432},{64,..., dimensions={0} | all-to-all | bytes 327680 | tf_op jit(solution)/shard_map/all_to_all | solution.py:254
  97.9 8.3 %all_to_all.28 = f32[4,80,128]{2,1,0:T(8,128)S(1)} all-to-all(f32[4,80,128]{2,1,0:T(8,128)S(1)} %broadcast_in_dim.10), channel_id=1, replica_groups={{0,32,64,96},{16,48,80,112},{128,160,192,224},{144,176,208,240},{256,28..., dimensions={0} | all-to-all | bytes 327680 | tf_op jit(solution)/shard_map/all_to_all | solution.py:251
  106.2 13.8 %all_to_all.29 = f32[16,80,128]{2,1,0:T(8,128)S(1)} all-to-all(f32[16,80,128]{2,1,0:T(8,128)S(1)} %broadcast_in_dim.11), channel_id=1, replica_groups=mesh['row'=32,'col'=16] {'col'}, dimensions={0} | all-to-all | bytes 1310720 | tf_op jit(solution)/shard_map/all_to_all | solution.py:248
  120.0 14.8 %basis.1 = (f32[48,512]{1,0:T(8,128)S(1)}, f32[48,512]{1,0:T(8,128)S(1)}) custom-call(f32[1280,128]{1,0:T(8,128)S(1)} %bitcast.4, f32[96,512]{1,0:T(8,128)S(1)} %get-tuple-element.18.rows_ref), custom_call_target="tpu_custom_call" | custom-call | tf_op jit(solution)/shard_map/basis/pallas_call | solution.py:101
  134.8 8.1 %collective-permute-start.1 = (f32[48,512]{1,0:T(8,128)S(1)}, f32[48,512]{1,0:T(8,128)S(1)}, u32[]{:S(2)}, u32[]{:S(2)}) collective-permute-start(f32[48,512]{1,0:T(8,128)S(1)} %get-tuple-element.20), channel_id=1, source_target_pairs={{0,16},{16,0},{32,48},{48,32},{64,80},{80,64},{96,112},{112,96},{1... | collective-permute-start | bytes 294920 | tf_op jit(solution)/shard_map/ppermute | solution.py:272
  142.9 0.9 collective-permute-done.1.back_ref
  143.9 0.7 merge.1
  (6 shorter events, 0.1 us)
Async XLA Ops:
  49.1 5.5 %collective-permute-start = (f32[48,512]{1,0:T(8,128)S(1)}, f32[48,512]{1,0:T(8,128)S(1)}, u32[]{:S(2)}, u32[]{:S(2)}) collective-permute-start(f32[48,512]{1,0:T(8,128)S(1)} %get-tuple-element.16), channel_id=1, source_target_pairs={{0,16},{16,0},{32,48},{48,32},{64,80},{80,64},{96,112},{112,96},{1... | collective-permute-start | bytes 294920 | tf_op jit(solution)/shard_map/ppermute | solution.py:269
  134.8 9.1 %collective-permute-start.1 = (f32[48,512]{1,0:T(8,128)S(1)}, f32[48,512]{1,0:T(8,128)S(1)}, u32[]{:S(2)}, u32[]{:S(2)}) collective-permute-start(f32[48,512]{1,0:T(8,128)S(1)} %get-tuple-element.20), channel_id=1, source_target_pairs={{0,16},{16,0},{32,48},{48,32},{64,80},{80,64},{96,112},{112,96},{1... | collective-permute-start | bytes 294920 | tf_op jit(solution)/shard_map/ppermute | solution.py:272
